TPU v7x, 32 devices: a whole 2x2x4 slice. The times are simulated.
32 devices in a mesh: rep: 2 (over core), shard: 16 (over z, y, x).
Axes of the slice: x: 2, y: 2, z: 4, core: 2. Of those that a mesh axis runs over, the one named last changes fastest.
Arguments:
- text_rows: bfloat16 [64, 512, 768], P(('rep', 'shard')), may hold values from -6 to 6
- slot_ids: int32 [64, 512], P(('rep', 'shard')), may hold values from 0 to 128, as said below
- seg_count: int32 [64], P(('rep', 'shard')), may hold values from 5 to 128, as said below
- w_qkv: bfloat16 [768, 2304], P('shard'), may hold values from -0.21875 to 0.21875
- qv_bias: bfloat16 [1536], P('shard'), may hold values from -3 to 3
- w_out: bfloat16 [768, 768], P('shard'), may hold values from -0.625 to 0.625
- out_bias: bfloat16 [768], P('shard'), may hold values from -3 to 3
- ln1_gain: bfloat16 [768], P('shard'), may hold values from 0.5 to 1.5
- ln1_shift: bfloat16 [768], P('shard'), may hold values from -3 to 3
- w_up: bfloat16 [768, 3072], P('shard'), may hold values from -0.21875 to 0.21875
- up_bias: bfloat16 [3072], P('shard'), may hold values from -3 to 3
- w_down: bfloat16 [3072, 768], P('shard'), may hold values from -0.109375 to 0.109375
- down_bias: bfloat16 [768], P('shard'), may hold values from -3 to 3
- ln2_gain: bfloat16 [768], P('shard'), may hold values from 0.5 to 1.5
- ln2_shift: bfloat16 [768], P('shard'), may hold values from -3 to 3
- cotangent: bfloat16 [64, 640, 768], P(('rep', 'shard')), may hold values from -6 to 6
Outputs:
- layer_out: bfloat16 [64, 640, 768], P(('rep', 'shard'))
- grad_text: float32 [64, 512, 768], P(('rep', 'shard'))
- grad_w_qkv: float32 [768, 2304], P('shard')
- grad_qv_bias: float32 [1536], P('shard')
- grad_w_out: float32 [768, 768], P('shard')
- grad_out_bias: float32 [768], P('shard')
- grad_ln1_gain: float32 [768], P('shard')
- grad_ln1_shift: float32 [768], P('shard')
- grad_w_up: float32 [768, 3072], P('shard')
- grad_up_bias: float32 [3072], P('shard')
- grad_w_down: float32 [3072, 768], P('shard')
- grad_down_bias: float32 [768], P('shard')
- grad_ln2_gain: float32 [768], P('shard')
- grad_ln2_shift: float32 [768], P('shard')
Inputs may be any that keep to these rules, and one draw needn't show every extreme that they name: `seg_count`: one document has exactly 128 segments. `slot_ids`: 128 marks a text row in no segment; any other value is below its document's seg_count.
All inputs are finite; a program needn't handle non-finite values.
Results may differ from a plain program's by a relative error of at most 0.012.
The roundings to bfloat16 on the way count: a program that leaves them out, or rounds other values in their place, can miss the bound.
Values may be sent and summed in bfloat16 or wider, within the bound.
No kernel may reach another device: no remote copies, remote signals or barrier semaphores. Data moves between devices by JAX's collectives and lax.ppermute only.
A program may use at most 192 MiB of HBM per device.

v0:
```python
from functools import partial

import jax
import jax.numpy as jnp
from jax import lax
from jax.sharding import PartitionSpec as P

HEADS = 12
SLOTS = 128


layer_eps = 1e-05
score_scale = 0.125
masked_score = -1000000000.0


def norm_forward(values, gain_vec, shift_vec):
    average = jnp.mean(values, axis=-1, keepdims=True)
    centred = values - average
    inverse = lax.rsqrt(jnp.mean(centred * centred, axis=-1, keepdims=True) + layer_eps)
    scaled = centred * inverse
    return (scaled * gain_vec + shift_vec, scaled, inverse)


def norm_backward(grad_norm, gain_vec, scaled, inverse):
    grad_scaled = grad_norm * gain_vec
    grad_mean = jnp.mean(grad_scaled, axis=-1, keepdims=True)
    second = jnp.mean(grad_scaled * scaled, axis=-1, keepdims=True)
    return inverse * (grad_scaled - grad_mean - scaled * second)


def score_block(queries, key_rows, key_live):
    scores = (
        jnp.einsum("qhc,khc->hqk", queries, key_rows, preferred_element_type=jnp.float32)
        * score_scale
    )
    return jnp.where(key_live[None, None, :], scores, masked_score)


def attend(bundle):
    queries, key_rows, value_rows, key_live = bundle
    scores = score_block(queries, key_rows, key_live)
    row_top = jnp.max(scores, axis=-1, keepdims=True)
    log_total = row_top + jnp.log(jnp.sum(jnp.exp(scores - row_top), axis=-1, keepdims=True))
    attn_probs = jnp.exp(scores - log_total).astype(jnp.bfloat16)
    context = jnp.einsum("hqk,khc->qhc", attn_probs, value_rows, preferred_element_type=jnp.float32)
    return (context.astype(jnp.bfloat16), log_total)


def attend_back(bundle):
    queries, key_rows, value_rows, key_live, log_total, grad_context = bundle
    scores = score_block(queries, key_rows, key_live)
    attn_probs = jnp.exp(scores - log_total)
    grad_probs = jnp.einsum(
        "qhc,khc->hqk", grad_context, value_rows, preferred_element_type=jnp.float32
    )
    row_dot = jnp.sum(attn_probs * grad_probs, axis=-1, keepdims=True)
    grad_scores = (attn_probs * (grad_probs - row_dot)).astype(jnp.bfloat16)
    grad_queries = (
        jnp.einsum("hqk,khc->qhc", grad_scores, key_rows, preferred_element_type=jnp.float32)
        * score_scale
    )
    grad_keys = (
        jnp.einsum("hqk,qhc->khc", grad_scores, queries, preferred_element_type=jnp.float32)
        * score_scale
    )
    grad_values = jnp.einsum(
        "hqk,qhc->khc",
        attn_probs.astype(jnp.bfloat16),
        grad_context,
        preferred_element_type=jnp.float32,
    )
    return (grad_queries, grad_keys, grad_values)


def body(
    text_rows,
    slot_ids,
    seg_count,
    w_qkv,
    qv_bias,
    w_out,
    out_bias,
    ln1_gain,
    ln1_shift,
    w_up,
    up_bias,
    w_down,
    down_bias,
    ln2_gain,
    ln2_shift,
    cotangent,
):
    shards = (
        w_qkv,
        w_out,
        w_up,
        w_down,
        qv_bias,
        out_bias,
        ln1_gain,
        ln1_shift,
        up_bias,
        down_bias,
        ln2_gain,
        ln2_shift,
    )
    gathered = (
        lax.all_gather(w_qkv, "shard", axis=0, tiled=True),
        lax.all_gather(w_out, "shard", axis=0, tiled=True),
        lax.all_gather(w_up, "shard", axis=0, tiled=True),
        lax.all_gather(w_down, "shard", axis=0, tiled=True),
        lax.all_gather(qv_bias, "shard", axis=0, tiled=True),
        lax.all_gather(out_bias, "shard", axis=0, tiled=True),
        lax.all_gather(ln1_gain, "shard", axis=0, tiled=True),
        lax.all_gather(ln1_shift, "shard", axis=0, tiled=True),
        lax.all_gather(up_bias, "shard", axis=0, tiled=True),
        lax.all_gather(down_bias, "shard", axis=0, tiled=True),
        lax.all_gather(ln2_gain, "shard", axis=0, tiled=True),
        lax.all_gather(ln2_shift, "shard", axis=0, tiled=True),
    )
    full_qkv, full_out, full_up, full_down = (gathered[0], gathered[1], gathered[2], gathered[3])
    small_set = tuple((member.astype(jnp.float32) for member in gathered[4:]))
    bias_qv, bias_out, gain_one, shift_one, bias_up, bias_down, gain_two, shift_two = small_set
    docs_here, text_len, model_width = text_rows.shape
    row_count = text_len + SLOTS
    head_count = HEADS
    head_size = model_width // head_count
    slot_range = jnp.arange(SLOTS, dtype=jnp.int32)
    one_hot = (slot_ids[:, None, :] == slot_range[None, :, None]).astype(jnp.bfloat16)
    members = jnp.sum(one_hot.astype(jnp.float32), axis=2)[:, :, None]
    divisor = jnp.sqrt(jnp.maximum(members, 1.0))
    summed = jnp.einsum("dst,dtc->dsc", one_hot, text_rows, preferred_element_type=jnp.float32)
    pooled = (summed / divisor).astype(jnp.bfloat16)
    joined = jnp.concatenate([text_rows, pooled], axis=1).reshape(
        docs_here * row_count, model_width
    )
    key_live = jnp.concatenate(
        [jnp.ones((docs_here, text_len), jnp.bool_), slot_range[None, :] < seg_count[:, None]],
        axis=1,
    )
    full_bias = jnp.concatenate(
        [bias_qv[:model_width], jnp.zeros((model_width,), jnp.float32), bias_qv[model_width:]]
    )
    projected = (jnp.dot(joined, full_qkv, preferred_element_type=jnp.float32) + full_bias).astype(
        jnp.bfloat16
    )
    split_rows = projected.reshape(docs_here, row_count, 3, head_count, head_size)
    queries = split_rows[:, :, 0]
    key_rows = split_rows[:, :, 1]
    value_rows = split_rows[:, :, 2]
    context, log_total = lax.map(attend, (queries, key_rows, value_rows, key_live))
    context = context.reshape(docs_here * row_count, model_width)
    attn_branch = jnp.dot(context, full_out, preferred_element_type=jnp.float32) + bias_out
    normed1, scaled_one, inverse_one = norm_forward(
        joined.astype(jnp.float32) + attn_branch, gain_one, shift_one
    )
    normed_low = normed1.astype(jnp.bfloat16)
    up_out = jnp.dot(normed_low, full_up, preferred_element_type=jnp.float32) + bias_up
    gelu_exact = partial(jax.nn.gelu, approximate=False)
    active_float, gelu_back = jax.vjp(gelu_exact, up_out)
    active = active_float.astype(jnp.bfloat16)
    down_out = jnp.dot(active, full_down, preferred_element_type=jnp.float32) + bias_down
    result, scaled_two, inverse_two = norm_forward(normed1 + down_out, gain_two, shift_two)
    layer_out = result.astype(jnp.bfloat16).reshape(docs_here, row_count, model_width)
    back_set = (
        lax.all_gather(shards[0], "shard", axis=0, tiled=True),
        lax.all_gather(shards[1], "shard", axis=0, tiled=True),
        lax.all_gather(shards[2], "shard", axis=0, tiled=True),
        lax.all_gather(shards[3], "shard", axis=0, tiled=True),
        lax.all_gather(shards[4], "shard", axis=0, tiled=True),
        lax.all_gather(shards[5], "shard", axis=0, tiled=True),
        lax.all_gather(shards[6], "shard", axis=0, tiled=True),
        lax.all_gather(shards[7], "shard", axis=0, tiled=True),
        lax.all_gather(shards[8], "shard", axis=0, tiled=True),
        lax.all_gather(shards[9], "shard", axis=0, tiled=True),
        lax.all_gather(shards[10], "shard", axis=0, tiled=True),
        lax.all_gather(shards[11], "shard", axis=0, tiled=True),
    )
    back_qkv, back_out, back_up, back_down = (back_set[0], back_set[1], back_set[2], back_set[3])
    grad_final = cotangent.astype(jnp.float32).reshape(docs_here * row_count, model_width)
    grad_gain_two = jnp.sum(grad_final * scaled_two, axis=0)
    grad_shift_two = jnp.sum(grad_final, axis=0)
    grad_resid2 = norm_backward(grad_final, gain_two, scaled_two, inverse_two)
    grad_down = grad_resid2.astype(jnp.bfloat16)
    grad_down_bias = jnp.sum(grad_down.astype(jnp.float32), axis=0)
    grad_w_down = jnp.dot(active.T, grad_down, preferred_element_type=jnp.float32)
    grad_active = jnp.dot(grad_down, back_down.T, preferred_element_type=jnp.float32)
    grad_up = gelu_back(grad_active)[0].astype(jnp.bfloat16)
    grad_up_bias = jnp.sum(grad_up.astype(jnp.float32), axis=0)
    grad_w_up = jnp.dot(normed_low.T, grad_up, preferred_element_type=jnp.float32)
    grad_normed1 = grad_resid2 + jnp.dot(grad_up, back_up.T, preferred_element_type=jnp.float32)
    grad_gain_one = jnp.sum(grad_normed1 * scaled_one, axis=0)
    grad_shift_one = jnp.sum(grad_normed1, axis=0)
    grad_resid1 = norm_backward(grad_normed1, gain_one, scaled_one, inverse_one)
    grad_attn = grad_resid1.astype(jnp.bfloat16)
    grad_out_bias = jnp.sum(grad_attn.astype(jnp.float32), axis=0)
    grad_w_out = jnp.dot(context.T, grad_attn, preferred_element_type=jnp.float32)
    grad_context = jnp.dot(grad_attn, back_out.T, preferred_element_type=jnp.float32).astype(
        jnp.bfloat16
    )
    grad_context = grad_context.reshape(docs_here, row_count, head_count, head_size)
    grad_queries, grad_keys, grad_values = lax.map(
        attend_back, (queries, key_rows, value_rows, key_live, log_total, grad_context)
    )
    grad_projected = jnp.stack([grad_queries, grad_keys, grad_values], axis=2).astype(jnp.bfloat16)
    grad_projected = grad_projected.reshape(docs_here * row_count, 3 * model_width)
    bias_sums = jnp.sum(grad_projected.astype(jnp.float32), axis=0)
    grad_qv_bias = jnp.concatenate([bias_sums[:model_width], bias_sums[2 * model_width :]])
    grad_w_qkv = jnp.dot(joined.T, grad_projected, preferred_element_type=jnp.float32)
    grad_joined = (
        jnp.dot(grad_projected, back_qkv.T, preferred_element_type=jnp.float32) + grad_resid1
    )
    grad_joined = grad_joined.reshape(docs_here, row_count, model_width)
    grad_summed = (grad_joined[:, text_len:] / divisor).astype(jnp.bfloat16)
    pool_back = jnp.einsum("dst,dsc->dtc", one_hot, grad_summed, preferred_element_type=jnp.float32)
    grad_text = grad_joined[:, :text_len] + pool_back
    partial_owned = (
        lax.psum_scatter(grad_w_qkv, "shard", scatter_dimension=0, tiled=True),
        lax.psum_scatter(grad_qv_bias, "shard", scatter_dimension=0, tiled=True),
        lax.psum_scatter(grad_w_out, "shard", scatter_dimension=0, tiled=True),
        lax.psum_scatter(grad_out_bias, "shard", scatter_dimension=0, tiled=True),
        lax.psum_scatter(grad_gain_one, "shard", scatter_dimension=0, tiled=True),
        lax.psum_scatter(grad_shift_one, "shard", scatter_dimension=0, tiled=True),
        lax.psum_scatter(grad_w_up, "shard", scatter_dimension=0, tiled=True),
        lax.psum_scatter(grad_up_bias, "shard", scatter_dimension=0, tiled=True),
        lax.psum_scatter(grad_w_down, "shard", scatter_dimension=0, tiled=True),
        lax.psum_scatter(grad_down_bias, "shard", scatter_dimension=0, tiled=True),
        lax.psum_scatter(grad_gain_two, "shard", scatter_dimension=0, tiled=True),
        lax.psum_scatter(grad_shift_two, "shard", scatter_dimension=0, tiled=True),
    )
    owned = lax.psum(
        (
            partial_owned[0],
            partial_owned[1],
            partial_owned[2],
            partial_owned[3],
            partial_owned[4],
            partial_owned[5],
            partial_owned[6],
            partial_owned[7],
            partial_owned[8],
            partial_owned[9],
            partial_owned[10],
            partial_owned[11],
        ),
        "rep",
    )
    return (
        layer_out,
        grad_text,
        owned[0],
        owned[1],
        owned[2],
        owned[3],
        owned[4],
        owned[5],
        owned[6],
        owned[7],
        owned[8],
        owned[9],
        owned[10],
        owned[11],
    )


def solution(mesh):
    in_specs = (
        P(("rep", "shard"), None, None),
        P(("rep", "shard"), None),
        P(("rep", "shard")),
        P("shard", None),
        P("shard"),
        P("shard", None),
        P("shard"),
        P("shard"),
        P("shard"),
        P("shard", None),
        P("shard"),
        P("shard", None),
        P("shard"),
        P("shard"),
        P("shard"),
        P(("rep", "shard"), None, None),
    )
    out_specs = (
        P(("rep", "shard"), None, None),
        P(("rep", "shard"), None, None),
        P("shard", None),
        P("shard"),
        P("shard", None),
        P("shard"),
        P("shard"),
        P("shard"),
        P("shard", None),
        P("shard"),
        P("shard", None),
        P("shard"),
        P("shard"),
        P("shard"),
    )
    return jax.shard_map(body, mesh=mesh, in_specs=in_specs, out_specs=out_specs, check_vma=False)
```

profile of v0, /device:TPU:0, one launch (start us, length us, event | category | flops | bytes accessed | tf_op | source)
XLA Modules:
  0.0 1132.9 jit_solution(5957142495723507579)
XLA Ops:
  22.3 79.4 %all-reduce.20 = (bf16[1536]{0:T(1024)(128)(2,1)S(1)}, bf16[768]{0:T(1024)(128)(2,1)S(1)}, bf16[768]{0:T(1024)(128)(2,1)S(1)}, bf16[768]{0:T(1024)(128)(2,1)S(1)...) all-reduce(bf16[1536]{0:T(1024)(128)(2,1)S(1)} %dynamic-update-slic, ...), channel_id=1, replica_groups=mesh['rep'=2,'shard'=16] {'shard'}, use_global_device_ids=true, to_apply=%add.1 | all-reduce | flops 9216 | bytes 36864
  128.1 12.2 %reshape.160 = bf16[2,640,3,12,64]{1,0,4,3,2:T(2,128)(2,1)} reshape(bf16[1280,2304]{0,1:T(8,128)(2,1)} %copy.60) | data formatting | bytes 11796480 | tf_op jit(solution)/shard_map/reshape | solution.py:148
  150.1 83.8 %while.26 = (s32[]{:T(128)}, bf16[2,640,12,64]{1,3,2,0:T(8,128)(2,1)}, f32[2,12,640,1]{2,1,3,0:T(8,128)}, bf16[2,640,12,64]{1,3,2,0:T(8,128)(2,1)}, pred[2,640]{...) while((s32[]{:T(128)}, ...), condition=%wide.region_4.5_spmd, body=%wide.region_1.4_spmd.sunk | while | flops 1312842240 | bytes 63176292 | solution.py:152
  150.4 12.0 %fusion.120 = (f32[12,640]{1,0:T(8,128)S(1)}, f32[12,640,640]{1,2,0:T(8,128)}) fusion(pred[640]{0:T(1024)(128)(4,1)S(1)} %dynamic-slice_reduce_fusion.4, bf16[2,640,12,64]{1,3,2,0:T(8,128)(2,1)S(1)} %get-tuple-element.397, s32[]{:T(128)S(6)} %copy.94, bf16[2,640,12,64]{1,3,2,0:T(8,128)(2,1)} %get-tuple-element.396), kind=kOutput, calls=%fused_computation.3.clone.1 | convolution fusion | flops 643883520 | bytes 21659648 | tf_op jit(solution)/shard_map/while/body/eval_jaxpr/qhc,khc->hqk/dot_general | solution.py:34
  173.7 12.5 %fusion.121 = bf16[2,640,12,64]{1,3,2,0:T(8,128)(2,1)} fusion(bf16[2,640,12,64]{1,3,2,0:T(8,128)(2,1)} %get-tuple-element.384, s32[]{:T(128)S(6)} %copy.94, f32[12,640,640]{1,2,0:T(8,128)} %get-tuple-element.359, f32[12,640]{1,0:T(8,128)S(1)} %get-tuple-element.361, pred[640]{0:T(1024)(128)(4,1)S(1)} %dynamic-slice_reduce_fusion.4, ...), kind=kOutput, calls=%fused_computation.8.clone.1 | convolution fusion | flops 649297920 | bytes 21659264 | tf_op jit(solution)/shard_map/while/body/eval_jaxpr/hqk,khc->qhc/dot_general | solution.py:46
  186.2 12.5 %fusion.120 = (f32[12,640]{1,0:T(8,128)S(1)}, f32[12,640,640]{1,2,0:T(8,128)}) fusion(pred[640]{0:T(1024)(128)(4,1)S(1)} %dynamic-slice_reduce_fusion.4, bf16[2,640,12,64]{1,3,2,0:T(8,128)(2,1)S(1)} %get-tuple-element.397, s32[]{:T(128)S(6)} %copy.94, bf16[2,640,12,64]{1,3,2,0:T(8,128)(2,1)} %get-tuple-element.396), kind=kOutput, calls=%fused_computation.3.clone.1 | convolution fusion | flops 643883520 | bytes 21659648 | tf_op jit(solution)/shard_map/while/body/eval_jaxpr/qhc,khc->hqk/dot_general | solution.py:34
  210.0 12.6 %fusion.121 = bf16[2,640,12,64]{1,3,2,0:T(8,128)(2,1)} fusion(bf16[2,640,12,64]{1,3,2,0:T(8,128)(2,1)} %get-tuple-element.384, s32[]{:T(128)S(6)} %copy.94, f32[12,640,640]{1,2,0:T(8,128)} %get-tuple-element.359, f32[12,640]{1,0:T(8,128)S(1)} %get-tuple-element.361, pred[640]{0:T(1024)(128)(4,1)S(1)} %dynamic-slice_reduce_fusion.4, ...), kind=kOutput, calls=%fused_computation.8.clone.1 | convolution fusion | flops 649297920 | bytes 21659264 | tf_op jit(solution)/shard_map/while/body/eval_jaxpr/hqk,khc->qhc/dot_general | solution.py:46
  247.1 46.2 %multiply_convert_fusion.1 = (bf16[1280,3072]{1,0:T(8,128)(2,1)}, f32[1280,3072]{1,0:T(8,128)}, f32[1280,3072]{1,0:T(8,128)}) fusion(f32[3072]{0:T(1024)S(1)} %copy-done.35, bf16[768,3072]{1,0:T(8,128)(2,1)} %all-gather.9.cloned.1.call-done, f32[1280,768]{1,0:T(8,128)} %copy-done.6, f32[768]{0:T(1024)S(1)} %convert_element_type.117, ...), kind=kOutput, calls=%fused_computation.61 | convolution fusion | flops 6304235520 | bytes 48001024 | tf_op jit(solution)/shard_map/dot_general | solution.py:159
  293.3 14.0 %all-gather.11.cloned.1.call-done = bf16[3072,768]{1,0:T(8,128)(2,1)} async-done(((bf16[192,768]{1,0:T(8,128)(2,1)}), bf16[3072,768]{1,0:T(8,128)(2,1)}) %all-gather.11.cloned.1.call-update) | async-done | bytes 4718608 | tf_op jit(solution)/shard_map/all_gather | solution.py:112
  326.8 23.7 %convert_reduce_fusion = (f32[3072]{0:T(1024)}, bf16[1280,3072]{1,0:T(8,128)(2,1)}) fusion(f32[1280,3072]{1,0:T(8,128)} %get-tuple-element.234, bf16[3072,768]{1,0:T(8,128)(2,1)} %all-gather.11.cloned.1.call-done, f32[1280,768]{1,0:T(8,128)} %get-tuple-element.228, f32[1280,3072]{1,0:T(8,128)} %get-tuple-element.251, f32[3072]{0:T(1024)S(1)} %copy-done.35), kind=kOutput, calls=%fused_computation.59 | convolution fusion | flops 6107624448 | bytes 47996928 | tf_op jit(solution)/shard_map/dot_general | solution.py:188
  350.5 13.4 %multiply_reduce_fusion.1 = (f32[768]{0:T(1024)}, f32[1280]{0:T(1024)S(1)}, f32[1280]{0:T(1024)S(1)}, f32[768]{0:T(1024)}, f32[1280,768]{1,0:T(8,128)S(1)}) fusion(f32[1280,768]{1,0:T(8,128)} %copy-done.6, f32[1280]{0:T(1024)S(1)} %add_rsqrt_fusion.1, f32[1280]{0:T(1024)S(1)} %broadcast_multiply_fusion.4, f32[768]{0:T(1024)S(1)} %convert_element_type.116, ...), kind=kOutput, calls=%fused_computation.91 | convolution fusion | flops 6049624064 | bytes 24409088 | tf_op jit(solution)/shard_map/dot_general | solution.py:192
  385.5 118.0 %while.27 = (s32[]{:T(128)}, bf16[2,640,12,64]{1,3,2,0:T(8,128)(2,1)}, bf16[2,640,12,64]{1,3,2,0:T(8,128)(2,1)}, bf16[2,640,12,64]{1,3,2,0:T(8,128)(2,1)}, bf16[...) while((s32[]{:T(128)}, ...), condition=%wide.region_15.16_spmd, body=%wide.region_13.15_spmd.sunk | while | flops 3220431360 | bytes 215530704 | solution.py:203
  396.5 12.6 %bitcast_dynamic-update-slice_fusion.11 = bf16[2,640,12,64]{1,3,2,0:T(8,128)(2,1)} fusion(bf16[2,640,12,64]{1,3,2,0:T(8,128)(2,1)} %get-tuple-element.413, s32[]{:T(128)S(6)} %copy.104, f32[12,640,640]{1,2,0:T(8,128)} %fusion.130, f32[12,640]{1,0:T(8,128)S(1)} %dynamic-slice_bitcast_fusion.2, pred[640]{0:T(1024)(128)(4,1)S(1)} %dynamic-slice_reduce_fusion.5, ...), kind=kOutput, calls=%fused_computation.29.clone.1 | convolution fusion | flops 648806400 | bytes 22652928 | tf_op jit(solution)/shard_map/while/body/eval_jaxpr/hqk,qhc->khc/dot_general | solution.py:67
  409.1 13.9 %multiply_reduce_fusion.7 = (f32[12,640]{1,0:T(8,128)S(1)}, f32[12,640,640]{1,2,0:T(8,128)}) fusion(f32[12,640,640]{1,2,0:T(8,128)} %fusion.130, f32[12,640]{1,0:T(8,128)S(1)} %dynamic-slice_bitcast_fusion.2, pred[640]{0:T(1024)(128)(4,1)S(1)} %dynamic-slice_reduce_fusion.5, bf16[2,640,12,64]{1,3,2,0:T(8,128)(2,1)S(1)} %copy-done.3, s32[]{:T(128)S(6)} %copy.104, ...), kind=kOutput, calls=%fused_computation.24.clone.1 | convolution fusion | flops 653713920 | bytes 41361408 | tf_op jit(solution)/shard_map/while/body/eval_jaxpr/qhc,khc->hqk/dot_general | solution.py:54
  423.0 15.1 %multiply_convert_fusion.3 = bf16[12,640,640]{1,2,0:T(8,128)(2,1)S(1)} fusion(f32[12,640,640]{1,2,0:T(8,128)} %get-tuple-element.373, f32[12,640,640]{1,2,0:T(8,128)} %fusion.130, f32[12,640]{1,0:T(8,128)S(1)} %get-tuple-element.374, f32[12,640]{1,0:T(8,128)S(1)} %dynamic-slice_bitcast_fusion.2, pred[640]{0:T(1024)(128)(4,1)S(1)} %dynamic-slice_reduce_fusion.5), kind=kLoop, calls=%fused_computation.23.clone.1 | loop fusion | flops 29491200 | bytes 49214080 | tf_op jit(solution)/shard_map/while/body/eval_jaxpr/convert_element_type | solution.py:58
  455.4 12.4 %bitcast_dynamic-update-slice_fusion.11 = bf16[2,640,12,64]{1,3,2,0:T(8,128)(2,1)} fusion(bf16[2,640,12,64]{1,3,2,0:T(8,128)(2,1)} %get-tuple-element.413, s32[]{:T(128)S(6)} %copy.104, f32[12,640,640]{1,2,0:T(8,128)} %fusion.130, f32[12,640]{1,0:T(8,128)S(1)} %dynamic-slice_bitcast_fusion.2, pred[640]{0:T(1024)(128)(4,1)S(1)} %dynamic-slice_reduce_fusion.5, ...), kind=kOutput, calls=%fused_computation.29.clone.1 | convolution fusion | flops 648806400 | bytes 22652928 | tf_op jit(solution)/shard_map/while/body/eval_jaxpr/hqk,qhc->khc/dot_general | solution.py:67
  467.8 13.8 %multiply_reduce_fusion.7 = (f32[12,640]{1,0:T(8,128)S(1)}, f32[12,640,640]{1,2,0:T(8,128)}) fusion(f32[12,640,640]{1,2,0:T(8,128)} %fusion.130, f32[12,640]{1,0:T(8,128)S(1)} %dynamic-slice_bitcast_fusion.2, pred[640]{0:T(1024)(128)(4,1)S(1)} %dynamic-slice_reduce_fusion.5, bf16[2,640,12,64]{1,3,2,0:T(8,128)(2,1)S(1)} %copy-done.3, s32[]{:T(128)S(6)} %copy.104, ...), kind=kOutput, calls=%fused_computation.24.clone.1 | convolution fusion | flops 653713920 | bytes 41361408 | tf_op jit(solution)/shard_map/while/body/eval_jaxpr/qhc,khc->hqk/dot_general | solution.py:54
  481.6 15.2 %multiply_convert_fusion.3 = bf16[12,640,640]{1,2,0:T(8,128)(2,1)S(1)} fusion(f32[12,640,640]{1,2,0:T(8,128)} %get-tuple-element.373, f32[12,640,640]{1,2,0:T(8,128)} %fusion.130, f32[12,640]{1,0:T(8,128)S(1)} %get-tuple-element.374, f32[12,640]{1,0:T(8,128)S(1)} %dynamic-slice_bitcast_fusion.2, pred[640]{0:T(1024)(128)(4,1)S(1)} %dynamic-slice_reduce_fusion.5), kind=kLoop, calls=%fused_computation.23.clone.1 | loop fusion | flops 29491200 | bytes 49214080 | tf_op jit(solution)/shard_map/while/body/eval_jaxpr/convert_element_type | solution.py:58
  525.6 12.8 %fusion.74 = f32[768,3072]{1,0:T(8,128)} fusion(bf16[1280,3072]{1,0:T(8,128)(2,1)} %get-tuple-element.256, f32[1280,768]{1,0:T(8,128)} %copy-done.6, f32[768]{0:T(1024)S(1)} %copy-done.39, f32[768]{0:T(1024)S(1)} %copy-done.29, f32[1280]{0:T(1024)S(1)} %copy-done.26, f32[1280]{0:T(1024)S(1)} %copy-done.22), kind=kOutput, calls=%fused_computation.141 | convolution fusion | flops 6044712960 | bytes 21250048 | tf_op jit(solution)/shard_map/dot_general | solution.py:191
  538.5 12.1 %fusion.71 = f32[3072,768]{1,0:T(8,128)} fusion(bf16[1280,3072]{1,0:T(8,128)(2,1)} %get-tuple-element.233, f32[1280,768]{1,0:T(8,128)} %get-tuple-element.228), kind=kOutput, calls=%fused_computation.138 | convolution fusion | flops 6040780800 | bytes 21233664 | tf_op jit(solution)/shard_map/dot_general | solution.py:187
  552.7 122.2 %reduce-scatter.5.cloned.1.call-done = f32[48,2304]{1,0:T(8,128)} async-done(((f32[768,2304]{1,0:T(8,128)}), f32[48,2304]{1,0:T(8,128)}) %reduce-scatter.5.cloned.1.call-update) | async-done | bytes 442384 | tf_op jit(solution)/shard_map/reduce_scatter | solution.py:219
  674.9 176.7 %reduce-scatter.9.cloned.1.call-done = f32[48,3072]{1,0:T(8,128)} async-done(((f32[768,3072]{1,0:T(8,128)}), f32[48,3072]{1,0:T(8,128)}) %reduce-scatter.9.cloned.1.call-update) | async-done | bytes 589840 | tf_op jit(solution)/shard_map/reduce_scatter | solution.py:225
  851.6 175.6 %reduce-scatter.11.cloned.1.call-done = f32[192,768]{1,0:T(8,128)} async-done(((f32[3072,768]{1,0:T(8,128)}), f32[192,768]{1,0:T(8,128)}) %reduce-scatter.11.cloned.1.call-update) | async-done | bytes 589840 | tf_op jit(solution)/shard_map/reduce_scatter | solution.py:227
  1027.5 75.4 %all-reduce.17 = (f32[1536]{0:T(1024)S(1)}, f32[768]{0:T(1024)S(1)}, f32[768]{0:T(1024)S(1)}, f32[768]{0:T(1024)S(1)}, f32[3072]{0:T(1024)S(1)}, /*index=5*/f32[...) all-reduce(f32[1536]{0:T(1024)S(1)} %pad_maximum_fusion.2, ...), channel_id=3, replica_groups=mesh['rep'=2,'shard'=16] {'shard'}, use_global_device_ids=true, to_apply=%region_19.20.clone | all-reduce | flops 9216 | bytes 73728
  (239 shorter events, 205.8 us)
Async XLA Ops:
  7.2 102.6 %copy-start.17 = (bf16[2,512,768]{2,1,0:T(8,128)(2,1)S(1)}, bf16[2,512,768]{2,1,0:T(8,128)(2,1)}, u32[]{:S(2)}) copy-start(bf16[2,512,768]{2,1,0:T(8,128)(2,1)} %param.20) | copy-start | bytes 4718596
  7.2 102.8 %all-gather.5.cloned.1.call-start = ((), (), s32[]{:S(2)}) async-start(), calls=%async_computation.4 | async-start | bytes 3760128 | tf_op jit(solution)/shard_map/all_gather | solution.py:109
  7.9 231.9 %all-gather.7.cloned.1.call-start = ((), (), s32[]{:S(2)}) async-start(), calls=%async_computation.5 | async-start | bytes 1253376 | tf_op jit(solution)/shard_map/all_gather | solution.py:110
  8.7 238.4 %all-gather.9.cloned.1.call-start = ((), (), s32[]{:S(2)}) async-start(), calls=%async_computation.6 | async-start | bytes 5013504 | tf_op jit(solution)/shard_map/all_gather | solution.py:111
  9.4 297.9 %all-gather.11.cloned.1.call-start = ((), (), s32[]{:S(2)}) async-start(), calls=%async_computation.7 | async-start | bytes 5013504 | tf_op jit(solution)/shard_map/all_gather | solution.py:112
  10.0 542.7 %reduce-scatter.7.cloned.1.call-start = ((), (), s32[]{:S(2)}) async-start(), calls=%async_computation.9 | async-start | bytes 2506752 | tf_op jit(solution)/shard_map/reduce_scatter | solution.py:221
  15.5 92.2 %copy-start.44 = (f32[2,128]{1,0:T(2,128)}, f32[2,128]{1,0:T(2,128)S(1)}, u32[]{:S(2)}) copy-start(f32[2,128]{1,0:T(2,128)S(1)} %maximum_sqrt_fusion) | copy-start | bytes 3076
  101.6 262.3 %copy-start.28 = (f32[768]{0:T(1024)}, f32[768]{0:T(1024)S(1)}, u32[]{:S(2)}) copy-start(f32[768]{0:T(1024)S(1)} %convert_element_type.116) | copy-start | bytes 9220
  101.6 205.6 %copy-start.38 = (f32[768]{0:T(1024)}, f32[768]{0:T(1024)S(1)}, u32[]{:S(2)}) copy-start(f32[768]{0:T(1024)S(1)} %convert_element_type.117) | copy-start | bytes 9220
  244.5 119.5 %copy-start.21 = (f32[1280]{0:T(1024)}, f32[1280]{0:T(1024)S(1)}, u32[]{:S(2)}) copy-start(f32[1280]{0:T(1024)S(1)} %broadcast_multiply_fusion.4) | copy-start | bytes 15364
  247.0 116.9 %copy-start.25 = (f32[1280]{0:T(1024)}, f32[1280]{0:T(1024)S(1)}, u32[]{:S(2)}) copy-start(f32[1280]{0:T(1024)S(1)} %add_rsqrt_fusion.1) | copy-start | bytes 15364
  247.0 60.3 %copy-start.40 = (f32[768]{0:T(1024)S(1)}, f32[768]{0:T(1024)}, u32[]{:S(2)}) copy-start(f32[768]{0:T(1024)} %convert_element_type.121) | copy-start | bytes 9220
  371.1 303.8 %reduce-scatter.5.cloned.1.call-start = ((), (), s32[]{:S(2)}) async-start(), calls=%async_computation.8 | async-start | bytes 7520256 | tf_op jit(solution)/shard_map/reduce_scatter | solution.py:219
  481.6 15.2 %copy-start.10 = (bf16[2,640,12,64]{1,3,2,0:T(8,128)(2,1)S(1)}, bf16[2,640,12,64]{1,3,2,0:T(8,128)(2,1)}, u32[]{:S(2)}) copy-start(bf16[2,640,12,64]{1,3,2,0:T(8,128)(2,1)} %get-tuple-element.412) | copy-start | bytes 5898244 | tf_op jit(solution)/shard_map/while
  524.9 326.7 %reduce-scatter.9.cloned.1.call-start = ((), (), s32[]{:S(2)}) async-start(), calls=%async_computation.10 | async-start | bytes 10027008 | tf_op jit(solution)/shard_map/reduce_scatter | solution.py:225
  538.5 488.8 %reduce-scatter.11.cloned.1.call-start = ((), (), s32[]{:S(2)}) async-start(), calls=%async_computation.11 | async-start | bytes 10027008 | tf_op jit(solution)/shard_map/reduce_scatter | solution.py:227
  550.6 476.8 %copy-start.30 = (f32[768]{0:T(1024)S(1)}, f32[768]{0:T(1024)}, u32[]{:S(2)}) copy-start(f32[768]{0:T(1024)} %get-tuple-element.229) | copy-start | bytes 9220
  550.6 476.8 %copy-start.32 = (f32[768]{0:T(1024)S(1)}, f32[768]{0:T(1024)}, u32[]{:S(2)}) copy-start(f32[768]{0:T(1024)} %get-tuple-element.161) | copy-start | bytes 9220
  550.6 476.8 %copy-start.33 = (f32[768]{0:T(1024)S(1)}, f32[768]{0:T(1024)}, u32[]{:S(2)}) copy-start(f32[768]{0:T(1024)} %get-tuple-element.227) | copy-start | bytes 9220
  550.6 476.8 %copy-start.34 = (f32[768]{0:T(1024)S(1)}, f32[768]{0:T(1024)}, u32[]{:S(2)}) copy-start(f32[768]{0:T(1024)} %get-tuple-element.157) | copy-start | bytes 9220
  550.6 476.8 %copy-start.36 = (f32[3072]{0:T(1024)S(1)}, f32[3072]{0:T(1024)}, u32[]{:S(2)}) copy-start(f32[3072]{0:T(1024)} %get-tuple-element.255) | copy-start | bytes 36868
  550.6 476.8 %copy-start.42 = (f32[768]{0:T(1024)S(1)}, f32[768]{0:T(1024)}, u32[]{:S(2)}) copy-start(f32[768]{0:T(1024)} %get-tuple-element.155) | copy-start | bytes 9220
  550.7 476.8 %copy-start.43 = (f32[768]{0:T(1024)S(1)}, f32[768]{0:T(1024)}, u32[]{:S(2)}) copy-start(f32[768]{0:T(1024)} %get-tuple-element.160) | copy-start | bytes 9220
  550.7 568.0 %all-reduce.23.cloned.1.call-start = ((), (), s32[]{:S(2)}) async-start(), calls=%async_computation.12 | async-start | bytes 3538944 | tf_op jit(solution)/shard_map/psum | solution.py:232
  (40 other events, 227.1 us)
Sparse Core Ops, SparseCore 0:
  10.8 74.7 all-gather.4
  88.4 54.8 all-gather.6
  146.1 79.3 all-gather.8
  228.1 79.1 all-gather.10
  371.2 126.0 reduce-scatter.6
  525.0 149.8 reduce-scatter.4
  681.5 170.0 reduce-scatter.8
  857.3 169.9 reduce-scatter.10
  1030.0 19.8 all-reduce.22
where the time goes:
time: 1140 us; the launch traced here: 1130 us
  waiting for transfers between devices  491 us (43%)
  matrix products  295 us (26%)
  blocking collectives  158 us (14%)
  local copies, waits for them, and re-layouts  82.8 us (7%)
  other arithmetic  74.5 us (7%)
  between operations  18.8 us (2%)
  loops' own time  12 us (1%)
    reduce_scatter x1, waiting for transfers between devices, body(): lax.psum_scatter(grad_w_up, 'shard', scatter_dimension=0, tiled=True)  177 us
    reduce_scatter x1, waiting for transfers between devices, body(): lax.psum_scatter(grad_w_down, 'shard', scatter_dimension=0, tiled=True)  176 us
    unnamed x2, blocking collectives  155 us
    reduce_scatter x1, waiting for transfers between devices, body(): lax.psum_scatter(grad_w_qkv, 'shard', scatter_dimension=0, tiled=True)  122 us
    dot_general x1, matrix products, body(): jnp.dot(normed_low, full_up, preferred_element_type=jnp.float32) + bias_up  46.2 us
    dot_general x4, matrix products, score_block(): jnp.einsum('qhc,khc->hqk', queries, key_rows, preferred_element_type=jnp....  46.2 us
    convert_element_type x2, other arithmetic, attend_back(): grad_scores = (attn_probs * (grad_probs - row_dot)).astype(jnp.bfloat16)  30.2 us
    dot_general x2, matrix products, attend_back(): jnp.einsum('qhc,khc->hqk', grad_context, value_rows, preferred_element_ty...  27.7 us
  transfers between devices with their start and end apart: 9, of which 4 were waited for; matrix products, arithmetic and copies ran while one was open for 33% of the time, Pallas kernels for 0%

commit v1 on v0

v1 whole, which is shorter than its diff:
```python
import math
from functools import partial

import jax
import jax.numpy as jnp
from jax import lax
from jax.experimental import pallas as pl
from jax.experimental.pallas import tpu as pltpu
from jax.sharding import PartitionSpec as P

HEADS = 12
SLOTS = 128
GROUPS = 3

layer_eps = 1e-05
score_scale = 0.125
masked_score = -1000000000.0
BF = jnp.bfloat16
F32 = jnp.float32
VMEM_LIMIT = 60 * 1024 * 1024

NT = (((1,), (1,)), ((), ()))
NN = (((1,), (0,)), ((), ()))
TN = (((0,), (0,)), ((), ()))


def mm(left, right, dims=NN):
    return lax.dot_general(left, right, dims, preferred_element_type=F32)


def params():
    return pltpu.CompilerParams(vmem_limit_bytes=VMEM_LIMIT)


def any_spec():
    return pl.BlockSpec(memory_space=pl.ANY)


def smem_spec():
    return pl.BlockSpec(memory_space=pltpu.SMEM)


def vmem_spec():
    return pl.BlockSpec(memory_space=pltpu.VMEM)


def halves_of(count):
    return 1 if count == 1 else 2


def load_pieces(piece_refs, place_ref, buf, sem, parts):
    whole = 2 // halves_of(place_ref.shape[1])
    at = 0
    for ref in piece_refs:
        rows = ref.shape[1]
        for i in range(ref.shape[0]):
            row = pl.multiple_of(place_ref[0, at] * rows, 16)
            for col, n, first in parts:
                col, n = col * whole, n * whole
                to = pl.multiple_of(place_ref[1, at] * n + first, 128)
                pltpu.make_async_copy(
                    ref.at[i, :, pl.ds(col, n)], buf.at[pl.ds(row, rows), pl.ds(to, n)], sem
                ).start()
            at += 1


def wait_all(buf, sem):
    pltpu.make_async_copy(buf, buf, sem).wait()


def store_pieces(buf, out_ref, place_ref, sem, n, col):
    rows = out_ref.shape[1]
    for i in range(out_ref.shape[0]):
        row = pl.multiple_of(place_ref[0, i] * rows, 16)
        at = pl.multiple_of(place_ref[1, i] * n, 128)
        pltpu.make_async_copy(
            buf.at[pl.ds(row, rows), pl.ds(at, n)], out_ref.at[i, :, pl.ds(col, n)], sem
        ).start()


def store_half(buf, out_ref, place_ref, sem, half, col):
    rows, n = out_ref.shape[1], buf.shape[1]
    count = out_ref.shape[0] // halves_of(out_ref.shape[0])
    first = (place_ref[1, 0] ^ half) * count
    for i in range(count):
        row = pl.multiple_of(place_ref[0, first + i] * rows, 16)
        pltpu.make_async_copy(
            buf.at[pl.ds(row, rows), :], out_ref.at[first + i, :, pl.ds(col, n)], sem
        ).start()


QKV_PARTS = tuple((g * 384, 384, g * 768) for g in range(GROUPS))


def mid_parts(width, ff):
    return ((0, width // 2, 0), (width // 2, ff // 2, width))


def norm_parts(values):
    average = jnp.mean(values, axis=-1, keepdims=True)
    centred = values - average
    inverse = lax.rsqrt(jnp.mean(centred * centred, axis=-1, keepdims=True) + layer_eps)
    return centred * inverse, inverse


def norm_backward(grad_norm, gain_vec, scaled, inverse):
    grad_scaled = grad_norm * gain_vec
    grad_mean = jnp.mean(grad_scaled, axis=-1, keepdims=True)
    second = jnp.mean(grad_scaled * scaled, axis=-1, keepdims=True)
    return inverse * (grad_scaled - grad_mean - scaled * second)


def put_sums(acc, sums_ref):
    sums_ref[...] = jnp.zeros_like(sums_ref)
    for i in range(acc.shape[0]):
        sums_ref[i : i + 1, :] = jnp.sum(acc[i], axis=0, keepdims=True)


def fold_rows(values):
    rows, cols = values.shape
    return jnp.sum(values.reshape(rows // 8, 8, cols), axis=0)


def one_hot_of(ids_row, dtype):
    slot = lax.broadcasted_iota(jnp.int32, (SLOTS, ids_row.shape[1]), 0)
    return jnp.where(slot == ids_row, 1.0, 0.0).astype(dtype)


def divisor_of(ids_row):
    members = jnp.sum(one_hot_of(ids_row, F32), axis=1, keepdims=True)
    return jnp.sqrt(jnp.maximum(members, 1.0))


def pool_kernel(ids_ref, text_ref, joined_ref):
    text_len = text_ref.shape[1]
    ids_row = ids_ref[0]
    summed = mm(one_hot_of(ids_row, BF), text_ref[0])
    joined_ref[0:text_len, :] = text_ref[0]
    joined_ref[text_len:, :] = (summed / divisor_of(ids_row)).astype(BF)


def pool(slot_ids, text_rows):
    docs, text_len, width = text_rows.shape
    rows = text_len + SLOTS
    return pl.pallas_call(
        pool_kernel,
        out_shape=jax.ShapeDtypeStruct((docs * rows, width), BF),
        grid=(docs,),
        in_specs=[
            pl.BlockSpec((1, 1, text_len), lambda d: (d, 0, 0)),
            pl.BlockSpec((1, text_len, width), lambda d: (d, 0, 0)),
        ],
        out_specs=pl.BlockSpec((rows, width), lambda d: (d, 0)),
        compiler_params=params(),
        name="pool",
    )(slot_ids.reshape(docs, 1, text_len), text_rows)


def head_mask(e, width=128, size=64):
    lane = lax.broadcasted_iota(jnp.int32, (1, width), 1)
    return (lane // size) == e


def mask_keys(scores, count, text_len):
    slot = lax.broadcasted_iota(jnp.int32, (1, SLOTS), 1)
    tail = jnp.where(slot < count, scores[:, text_len:], masked_score)
    return jnp.concatenate([scores[:, :text_len], tail], axis=1)


def attn_fwd_kernel(docs, rows, n_arrays, *refs):
    place_ref, count_ref, joined_ref, bias_ref = refs[:4]
    pieces = refs[4 : 4 + n_arrays]
    proj_ref, ctx_ref, wbuf, sem = refs[4 + n_arrays :]
    g = pl.program_id(0)
    width = joined_ref.shape[1]
    span = width // GROUPS

    @pl.when(g == 0)
    def _():
        load_pieces(pieces, place_ref, wbuf, sem, QKV_PARTS)
        wait_all(wbuf, sem)

    cols = pl.ds(pl.multiple_of(g * width, 128), width)
    proj_ref[0] = (mm(joined_ref[...], wbuf[:, cols]) + bias_ref[:, cols]).astype(BF)

    def doc_step(d, carry):
        at = pl.ds(pl.multiple_of(d * rows, 128), rows)
        count = count_ref[d]
        for pair in range(span // 128):
            lo = 128 * pair
            first = 3 * lo
            queries = proj_ref[0, at, first : first + 128] * BF(score_scale)
            keys = proj_ref[0, at, first + 128 : first + 256]
            values = proj_ref[0, at, first + 256 : first + 384]
            total = None
            for e in range(2):
                mask = head_mask(e)
                scores = mm(jnp.where(mask, queries, BF(0)), keys, NT)
                scores = mask_keys(scores, count, rows - SLOTS)
                top = jnp.max(scores, axis=1, keepdims=True)
                weights = jnp.exp(scores - top)
                norm = 1.0 / jnp.sum(weights, axis=1, keepdims=True)
                probs = (weights * norm).astype(BF)
                part = mm(probs, jnp.where(mask, values, BF(0)))
                total = part if total is None else total + part
            ctx_ref[at, lo : lo + 128] = total.astype(BF)
        return carry

    lax.fori_loop(0, docs, doc_step, 0)


def attn_fwd(place, seg_count, joined, bias, pieces):
    docs = seg_count.shape[0]
    total, width = joined.shape
    rows = total // docs
    span = width // GROUPS
    return pl.pallas_call(
        partial(attn_fwd_kernel, docs, rows, len(pieces)),
        out_shape=(
            jax.ShapeDtypeStruct((GROUPS, total, width), BF),
            jax.ShapeDtypeStruct((total, width), BF),
        ),
        grid=(GROUPS,),
        in_specs=[smem_spec(), smem_spec(), vmem_spec(), vmem_spec()] + [any_spec()] * len(pieces),
        out_specs=(
            pl.BlockSpec((1, total, width), lambda g: (g, 0, 0)),
            pl.BlockSpec((total, span), lambda g: (0, g)),
        ),
        scratch_shapes=[pltpu.VMEM((width, 3 * width), BF), pltpu.SemaphoreType.DMA(())],
        compiler_params=params(),
        name="attn_fwd",
    )(place, seg_count, joined, bias, *pieces)


def up_kernel(n_arrays, *refs):
    place_ref, joined_ref, ctx_ref, obias_ref, gain_ref, shift_ref, ubias_ref = refs[:7]
    pieces = refs[7 : 7 + n_arrays]
    scaled_ref, inv_ref, act_ref, slope_ref, wbuf, sem = refs[7 + n_arrays :]
    width = joined_ref.shape[1]

    @pl.when(pl.program_id(0) == 0)
    def _():
        load_pieces(pieces, place_ref, wbuf, sem, mid_parts(width, wbuf.shape[1] - width))
        wait_all(wbuf, sem)

    branch = mm(ctx_ref[...], wbuf[:, :width]) + obias_ref[...]
    scaled, inverse = norm_parts(joined_ref[...].astype(F32) + branch)
    scaled_ref[...] = scaled
    inv_ref[...] = inverse
    low = (scaled * gain_ref[...] + shift_ref[...]).astype(BF)
    ff = act_ref.shape[1]
    step = 768
    for c in range(0, ff, step):
        up = mm(low, wbuf[:, width + c : width + c + step]) + ubias_ref[:, c : c + step]
        half = 0.5 + 0.5 * lax.erf(up * math.sqrt(0.5))
        act_ref[:, c : c + step] = (up * half).astype(BF)
        slope_ref[:, c : c + step] = half + up * (
            jnp.exp(-0.5 * (up * up)) * (1.0 / math.sqrt(2.0 * math.pi))
        )


def up_call(place, joined, ctx, obias, gain, shift, ubias, pieces, block=256):
    total, width = joined.shape
    ff = ubias.shape[1]
    row = lambda i: (i, 0)
    return pl.pallas_call(
        partial(up_kernel, len(pieces)),
        out_shape=(
            jax.ShapeDtypeStruct((total, width), F32),
            jax.ShapeDtypeStruct((total, 1), F32),
            jax.ShapeDtypeStruct((total, ff), BF),
            jax.ShapeDtypeStruct((total, ff), F32),
        ),
        grid=(total // block,),
        in_specs=[
            smem_spec(),
            pl.BlockSpec((block, width), row),
            pl.BlockSpec((block, width), row),
        ]
        + [vmem_spec()] * 4
        + [any_spec()] * len(pieces),
        out_specs=(
            pl.BlockSpec((block, width), row),
            pl.BlockSpec((block, 1), row),
            pl.BlockSpec((block, ff), row),
            pl.BlockSpec((block, ff), row),
        ),
        scratch_shapes=[pltpu.VMEM((width, width + ff), BF), pltpu.SemaphoreType.DMA(())],
        compiler_params=params(),
        name="up",
    )(place, joined, ctx, obias, gain, shift, ubias, *pieces)


def down_kernel(n_arrays, n_rows, n_cols, *refs):
    place_ref, scaled_ref, act_ref, cot_ref, gain1_ref, shift1_ref, dbias_ref, gain_ref, shift_ref = refs[:9]
    pieces = refs[9 : 9 + n_arrays]
    out_ref, resid_ref, sums_ref, gw_ref, wbuf, low_buf, gbuf, acc, sem, osem = refs[9 + n_arrays :]
    step = pl.program_id(0)
    block = cot_ref.shape[0]
    ff = wbuf.shape[0]
    tile = ff // n_cols

    @pl.when(step == 0)
    def _():
        load_pieces(pieces, place_ref, wbuf, sem, ((0, wbuf.shape[1] // 2 * halves_of(place_ref.shape[1]), 0),))
        acc[...] = jnp.zeros_like(acc)
        wait_all(wbuf, sem)

    @pl.when(step < n_rows)
    def _():
        at = pl.ds(pl.multiple_of(step * block, block), block)
        down = mm(act_ref[at, :], wbuf[...]) + dbias_ref[...]
        normed1 = scaled_ref[...] * gain1_ref[...] + shift1_ref[...]
        scaled2, inverse2 = norm_parts(normed1 + down)
        out_ref[...] = (scaled2 * gain_ref[...] + shift_ref[...]).astype(BF)
        grad = cot_ref[...].astype(F32)
        resid = norm_backward(grad, gain_ref[...], scaled2, inverse2)
        resid_ref[...] = resid
        low = resid.astype(BF)
        low_buf[at, :] = low
        acc[0] += fold_rows(grad * scaled2)
        acc[1] += fold_rows(grad)
        acc[2] += fold_rows(low.astype(F32))

    @pl.when(step >= n_rows)
    def _():
        c = step - n_rows
        cols = pl.ds(pl.multiple_of(c * tile, 128), tile)
        gbuf[cols, :] = mm(act_ref[:, cols], low_buf[...], TN).astype(BF)

    @pl.when(step == n_rows + n_cols - 1)
    def _():
        store_pieces(gbuf, gw_ref, place_ref, osem, gbuf.shape[1], 0)
        put_sums(acc, sums_ref)
        wait_all(gbuf, osem)


def down_call(place, scaled1, act, cot, gain1, shift1, dbias, gain, shift, pieces, block=256, tile=384):
    total, width = scaled1.shape
    ff = act.shape[1]
    n_rows, n_cols = total // block, ff // tile
    row = lambda i: (jnp.minimum(i, n_rows - 1), 0)
    count = place.shape[1]
    return pl.pallas_call(
        partial(down_kernel, len(pieces), n_rows, n_cols),
        out_shape=(
            jax.ShapeDtypeStruct((total, width), BF),
            jax.ShapeDtypeStruct((total, width), F32),
            jax.ShapeDtypeStruct((8, width), F32),
            jax.ShapeDtypeStruct((count, ff // count, width), BF),
        ),
        grid=(n_rows + n_cols,),
        in_specs=[smem_spec(), pl.BlockSpec((block, width), row), vmem_spec(), pl.BlockSpec((block, width), row)]
        + [vmem_spec()] * 5
        + [any_spec()] * len(pieces),
        out_specs=(
            pl.BlockSpec((block, width), row),
            pl.BlockSpec((block, width), row),
            pl.BlockSpec((8, width), lambda i: (0, 0)),
            any_spec(),
        ),
        scratch_shapes=[
            pltpu.VMEM((ff, width), BF),
            pltpu.VMEM((total, width), BF),
            pltpu.VMEM((ff, width), BF),
            pltpu.VMEM((3, 8, width), F32),
            pltpu.SemaphoreType.DMA(()),
            pltpu.SemaphoreType.DMA(()),
        ],
        compiler_params=params(),
        name="down",
    )(place, scaled1, act, cot, gain1, shift1, dbias, gain, shift, *pieces)


def ffn_back_kernel(n_up, n_down, n_rows, n_cols, *refs):
    (uplace_ref, dplace_ref, resid_ref, slope_ref, scaled_ref, inv_ref, ctx_ref, gain_ref, shift_ref) = refs[:9]
    ups = refs[9 : 9 + n_up]
    downs = refs[9 + n_up : 9 + n_up + n_down]
    (resid1_ref, gctx_ref, sums_ref, usum_ref, gw_ref) = refs[9 + n_up + n_down : 14 + n_up + n_down]
    wup, wdown, gup, low, gattn, gbuf, acc, uacc, sem, dsem, osem = refs[14 + n_up + n_down :]
    step = pl.program_id(0)
    block, width = resid_ref.shape
    ff = wdown.shape[0]
    tile = gbuf.shape[1]

    @pl.when(step == 0)
    def _():
        load_pieces(downs, dplace_ref, wdown, dsem, ((0, width // 2 * halves_of(dplace_ref.shape[1]), 0),))
        load_pieces(ups, uplace_ref, wup, sem, mid_parts(width, ff))
        acc[...] = jnp.zeros_like(acc)
        uacc[...] = jnp.zeros_like(uacc)
        wait_all(wdown, dsem)
        wait_all(wup, sem)

    @pl.when(step < n_rows)
    def _():
        at = pl.ds(pl.multiple_of(step * block, block), block)
        resid = resid_ref[...]
        gdown = resid.astype(BF)
        chunk = 768
        gnorm = resid
        for c in range(0, ff, chunk):
            gact = mm(gdown, wdown[c : c + chunk, :], NT)
            up = (gact * slope_ref[:, c : c + chunk]).astype(BF)
            gup[at, c : c + chunk] = up
            uacc[:, c : c + chunk] += fold_rows(up.astype(F32))
        gnorm = resid + mm(gup[at, :], wup[:, width:], NT)
        scaled = scaled_ref[...]
        acc[0] += fold_rows(gnorm * scaled)
        acc[1] += fold_rows(gnorm)
        resid1 = norm_backward(gnorm, gain_ref[...], scaled, inv_ref[...])
        resid1_ref[...] = resid1
        attn = resid1.astype(BF)
        gattn[at, :] = attn
        acc[2] += fold_rows(attn.astype(F32))
        low[at, :] = (scaled * gain_ref[...] + shift_ref[...]).astype(BF)
        gctx_ref[...] = mm(attn, wup[:, :width], NT).astype(BF)

    halves = halves_of(uplace_ref.shape[1])

    @pl.when(step == n_rows)
    def _():
        put_sums(acc, sums_ref)
        usum_ref[...] = jnp.sum(uacc[...], axis=0, keepdims=True)
        gbuf[...] = mm(ctx_ref[...], gattn[...], TN).astype(BF)
        store_pieces(gbuf, gw_ref, uplace_ref, osem, width // halves, 0)
        wait_all(gbuf, osem)

    @pl.when(step > n_rows)
    def _():
        c = step - n_rows - 1
        cols = pl.ds(pl.multiple_of(c * tile, 128), tile)
        gbuf[...] = mm(low[...], gup[:, cols], TN).astype(BF)
        per = n_cols // halves
        at = pl.multiple_of(width // halves + (c % per) * tile, 128)
        store_half(gbuf, gw_ref, uplace_ref, osem, c // per, at)
        wait_all(gbuf, osem)


def ffn_back(uplace, dplace, resid2, slope, scaled1, inv1, ctx, gain, shift, ups, downs, block=256):
    total, width = resid2.shape
    ff = slope.shape[1]
    n_rows = total // block
    n_cols = ff // width
    row = lambda i: (jnp.minimum(i, n_rows - 1), 0)
    count = uplace.shape[1]
    halves = halves_of(count)
    return pl.pallas_call(
        partial(ffn_back_kernel, len(ups), len(downs), n_rows, n_cols),
        out_shape=(
            jax.ShapeDtypeStruct((total, width), F32),
            jax.ShapeDtypeStruct((total, width), BF),
            jax.ShapeDtypeStruct((8, width), F32),
            jax.ShapeDtypeStruct((1, ff), F32),
            jax.ShapeDtypeStruct((count, width * halves // count, (width + ff) // halves), BF),
        ),
        grid=(n_rows + 1 + n_cols,),
        in_specs=[
            smem_spec(),
            smem_spec(),
            pl.BlockSpec((block, width), row),
            pl.BlockSpec((block, ff), row),
            pl.BlockSpec((block, width), row),
            pl.BlockSpec((block, 1), row),
            vmem_spec(),
            vmem_spec(),
            vmem_spec(),
        ]
        + [any_spec()] * (len(ups) + len(downs)),
        out_specs=(
            pl.BlockSpec((block, width), row),
            pl.BlockSpec((block, width), row),
            pl.BlockSpec((8, width), lambda i: (0, 0)),
            pl.BlockSpec((1, ff), lambda i: (0, 0)),
            any_spec(),
        ),
        scratch_shapes=[
            pltpu.VMEM((width, width + ff), BF),
            pltpu.VMEM((ff, width), BF),
            pltpu.VMEM((total, ff), BF),
            pltpu.VMEM((total, width), BF),
            pltpu.VMEM((total, width), BF),
            pltpu.VMEM((width, width), BF),
            pltpu.VMEM((3, 8, width), F32),
            pltpu.VMEM((8, ff), F32),
            pltpu.SemaphoreType.DMA(()),
            pltpu.SemaphoreType.DMA(()),
            pltpu.SemaphoreType.DMA(()),
        ],
        compiler_params=params(),
        name="ffn_back",
    )(uplace, dplace, resid2, slope, scaled1, inv1, ctx, gain, shift, *ups, *downs)


def attn_back_kernel(docs, rows, *refs):
    place_ref, count_ref, joined_ref, proj_ref, gctx_ref, gproj_ref, sums_ref, gw_ref, gbuf, osem = refs
    width = joined_ref.shape[1]
    span = width // GROUPS
    text_len = rows - SLOTS

    def doc_step(d, carry):
        at = pl.ds(pl.multiple_of(d * rows, 128), rows)
        count = count_ref[d]
        slot = lax.broadcasted_iota(jnp.int32, (SLOTS, 1), 0)
        for pair in range(span // 128):
            lo = 128 * pair
            first = 3 * lo
            queries = proj_ref[0, at, first : first + 128] * BF(score_scale)
            keys = proj_ref[0, at, first + 128 : first + 256]
            values = proj_ref[0, at, first + 256 : first + 384]
            grads = gctx_ref[at, lo : lo + 128]
            keys_low = keys * BF(score_scale)
            dq = dk = dv = None
            for e in range(2):
                mask = head_mask(e)
                q_e = jnp.where(mask, queries, BF(0))
                g_e = jnp.where(mask, grads, BF(0))
                k_e = jnp.where(mask, keys_low, BF(0))
                scores = mm(keys, q_e, NT)
                tail = jnp.where(slot < count, scores[text_len:, :], masked_score)
                scores = jnp.concatenate([scores[:text_len, :], tail], axis=0)
                top = jnp.max(scores, axis=0, keepdims=True)
                weights = jnp.exp(scores - top)
                probs = weights * (1.0 / jnp.sum(weights, axis=0, keepdims=True))
                gprobs = mm(values, g_e, NT)
                dot = jnp.sum(probs * gprobs, axis=0, keepdims=True)
                gscores = (probs * (gprobs - dot)).astype(BF)
                dv_e = mm(probs.astype(BF), g_e)
                dk_e = mm(gscores, q_e)
                dq_e = mm(k_e, gscores, TN)
                dq = dq_e if dq is None else dq + dq_e
                dk = dk_e if dk is None else dk + dk_e
                dv = dv_e if dv is None else dv + dv_e
            gproj_ref[0, at, first : first + 128] = dq.T.astype(BF)
            gproj_ref[0, at, first + 128 : first + 256] = dk.astype(BF)
            gproj_ref[0, at, first + 256 : first + 384] = dv.astype(BF)
        return carry

    lax.fori_loop(0, docs, doc_step, 0)
    sums_ref[0] = jnp.sum(gproj_ref[0].astype(F32), axis=0, keepdims=True)
    gbuf[...] = mm(joined_ref[...], gproj_ref[0], TN).astype(BF)
    n = width // halves_of(gw_ref.shape[0])
    store_pieces(gbuf, gw_ref, place_ref, osem, n, pl.multiple_of(pl.program_id(0) * n, 128))
    wait_all(gbuf, osem)


def attn_back(place, seg_count, joined, proj, gctx, first=0, groups=GROUPS):
    docs = seg_count.shape[0]
    total, width = joined.shape
    rows = total // docs
    span = width // GROUPS
    count = place.shape[1]
    halves = halves_of(count)
    return pl.pallas_call(
        partial(attn_back_kernel, docs, rows),
        out_shape=(
            jax.ShapeDtypeStruct((groups, total, width), BF),
            jax.ShapeDtypeStruct((groups, 1, width), F32),
            jax.ShapeDtypeStruct((count, width * halves // count, groups * width // halves), BF),
        ),
        grid=(groups,),
        in_specs=[
            smem_spec(),
            smem_spec(),
            vmem_spec(),
            pl.BlockSpec((1, total, width), lambda g: (first + g, 0, 0)),
            pl.BlockSpec((total, span), lambda g: (0, first + g)),
        ],
        out_specs=(
            pl.BlockSpec((1, total, width), lambda g: (g, 0, 0)),
            pl.BlockSpec((1, 1, width), lambda g: (g, 0, 0)),
            any_spec(),
        ),
        scratch_shapes=[pltpu.VMEM((width, width), BF), pltpu.SemaphoreType.DMA(())],
        compiler_params=params(),
        name="attn_back",
    )(place, seg_count, joined, proj, gctx)


def text_kernel(n_arrays, n_grads, *refs):
    place_ref, ids_ref, resid_ref = refs[:3]
    grads = refs[3 : 3 + n_grads]
    pieces = refs[3 + n_grads : 3 + n_grads + n_arrays]
    out_ref, wbuf, sem = refs[3 + n_grads + n_arrays :]
    width = wbuf.shape[0]
    text_len = out_ref.shape[1]

    @pl.when(pl.program_id(0) == 0)
    def _():
        load_pieces(pieces, place_ref, wbuf, sem, QKV_PARTS)
        wait_all(wbuf, sem)

    total = resid_ref[...]
    g = 0
    for ref in grads:
        for i in range(ref.shape[0]):
            total = total + mm(ref[i], wbuf[:, g * width : (g + 1) * width], NT)
            g += 1
    ids_row = ids_ref[0]
    summed = (total[text_len:, :] / divisor_of(ids_row)).astype(BF)
    out_ref[0] = total[:text_len, :] + mm(one_hot_of(ids_row, BF), summed, TN)


def text_grad(place, slot_ids, resid1, grads, pieces):
    docs, text_len = slot_ids.shape
    total, width = resid1.shape
    rows = total // docs
    return pl.pallas_call(
        partial(text_kernel, len(pieces), len(grads)),
        out_shape=jax.ShapeDtypeStruct((docs, text_len, width), F32),
        grid=(docs,),
        in_specs=[
            smem_spec(),
            pl.BlockSpec((1, 1, text_len), lambda d: (d, 0, 0)),
            pl.BlockSpec((rows, width), lambda d: (d, 0)),
        ]
        + [pl.BlockSpec((g.shape[0], rows, width), lambda d: (0, d, 0)) for g in grads]
        + [any_spec()] * len(pieces),
        out_specs=pl.BlockSpec((1, text_len, width), lambda d: (d, 0, 0)),
        scratch_shapes=[pltpu.VMEM((width, 3 * width), BF), pltpu.SemaphoreType.DMA(())],
        compiler_params=params(),
        name="text_grad",
    )(place, slot_ids.reshape(docs, 1, text_len), resid1, *grads, *pieces)


AXES = ("rep", "shard")
CHIPS = 16


def flips(core):
    return (1, 2) if core == 0 else (2, 1)


def pairs(flip_of):
    return [
        (core * CHIPS + s, core * CHIPS + (s ^ flip_of(core)))
        for core in range(2)
        for s in range(CHIPS)
    ]


Z_PERMS = [pairs(lambda core, k=k: k << 2) for k in (1, 2, 3)]
FIRST = pairs(lambda core: flips(core)[0])
SECOND = pairs(lambda core: flips(core)[1])
SWAP = [(core * CHIPS + s, (1 - core) * CHIPS + s) for core in range(2) for s in range(CHIPS)]


def send(array, perm):
    return lax.ppermute(array, AXES, perm)


def place_table(core, shard):
    order = jnp.arange(2 * CHIPS, dtype=jnp.int32)
    other, second, first, far = order // 16, (order // 8) % 2, (order // 4) % 2, order % 4
    half = core ^ other
    bits = jnp.where(half == 0, second * 2 + first, first * 2 + second)
    return jnp.stack([shard ^ (far * 4) ^ bits, half])


def gather(own):
    column = jnp.concatenate([own] + [send(own, perm) for perm in Z_PERMS], axis=0)
    first = send(column, FIRST)
    held = [column, first, send(column, SECOND), send(first, SECOND)]
    return held + [send(part, SWAP) for part in held]


def add(left, right):
    return (left.astype(F32) + right.astype(F32)).astype(BF)


def scatter(pieces):
    got = send(pieces[16:], SWAP)
    keep, away = add(pieces[:8], got[:8]), add(pieces[8:16], got[8:])
    got = send(away, SECOND)
    keep, away = add(keep[:4], got[:4]), add(keep[4:], got[4:])
    got = send(away, FIRST)
    own = keep[0].astype(F32) + got[0].astype(F32)
    total = own
    parts = add(keep[1:], got[1:])
    for k, perm in enumerate(Z_PERMS):
        total = total + send(parts[k], perm).astype(F32)
    return total


def join_cores(core, mine):
    theirs = send(mine, SWAP)
    return jnp.where(core == 0, mine, theirs), jnp.where(core == 0, theirs, mine)


def to_pairs(array):
    width = array.shape[1] // 3
    return jnp.concatenate(
        [array[:, t * width + p : t * width + p + 128] for p in range(0, width, 128) for t in range(3)],
        axis=1,
    )


def from_pairs(array):
    width = array.shape[1] // 3
    return jnp.concatenate(
        [array[:, 3 * p + t * 128 : 3 * p + t * 128 + 128] for t in range(3) for p in range(0, width, 128)],
        axis=1,
    )


def half_of(array, core):
    n = array.shape[1] // 2
    return lax.dynamic_slice_in_dim(array, core * n, n, 1)


def body(
    text_rows,
    slot_ids,
    seg_count,
    w_qkv,
    qv_bias,
    w_out,
    out_bias,
    ln1_gain,
    ln1_shift,
    w_up,
    up_bias,
    w_down,
    down_bias,
    ln2_gain,
    ln2_shift,
    cotangent,
):
    docs, text_len, width = text_rows.shape
    rows = text_len + SLOTS
    core = lax.axis_index("rep")
    shard = lax.axis_index("shard")
    chips = lax.axis_size("shard")
    small = (qv_bias, out_bias, ln1_gain, ln1_shift, up_bias, down_bias, ln2_gain, ln2_shift)
    sizes = [v.shape[0] for v in small]
    starts = [sum(sizes[:i]) for i in range(len(sizes))]
    packed = jnp.concatenate(small)
    staged = chips == CHIPS and lax.axis_size("rep") == 2
    joined = pool(slot_ids, text_rows)
    if staged:
        part = w_qkv.shape[0]
        lines = 640 // 128
        note = jnp.pad(packed, (0, 640 - packed.shape[0])).reshape(lines, 128)
        note = jnp.pad(note, ((0, part - lines), (0, 0)))
        own = [
            lax.dynamic_slice_in_dim(w_qkv, t * width + (2 * g + core) * 128, 128, 1)
            for g in range(GROUPS)
            for t in range(3)
        ]
        qkv = gather(jnp.concatenate(own + [note], axis=1)[None])
        mid = gather(jnp.concatenate([half_of(w_out, core), half_of(w_up, core)], axis=1)[None])
        part = w_down.shape[0] // 2
        down = gather(lax.dynamic_slice_in_dim(w_down, core * part, part, 0)[None])
        place = place_table(core, shard)
        notes = jnp.concatenate([p[:, :lines, 1152:] for p in qkv[:4]], axis=0)
        notes = notes.reshape(CHIPS, lines * 128).astype(F32)
        back = jnp.arange(CHIPS, dtype=jnp.int32)[:, None] == place[0, :CHIPS][None, :]
        table = jnp.dot(back.astype(F32), notes, precision=lax.Precision.HIGHEST)
        down_place = jnp.stack([2 * place[0] + place[1], jnp.zeros_like(place[1])])
    else:
        whole = lambda w: [lax.all_gather(w, "shard", axis=0, tiled=True)[None]]
        qkv, down = whole(to_pairs(w_qkv)), whole(w_down)
        mid = whole(jnp.concatenate([w_out, w_up], axis=1))
        place = down_place = jnp.zeros((2, 1), jnp.int32)
        table = lax.all_gather(packed[None], "shard", axis=0, tiled=True).astype(F32)
    full = [table[:, a : a + n].reshape(1, chips * n) for a, n in zip(starts, sizes)]
    bias_qv, bias_out, gain_one, shift_one, bias_up, bias_down, gain_two, shift_two = full
    full_bias = jnp.concatenate(
        [bias_qv[:, :width], jnp.zeros((1, width), F32), bias_qv[:, width:]], axis=1
    )
    proj, context = attn_fwd(place, seg_count, joined, to_pairs(full_bias), qkv)
    scaled_one, inverse_one, active, slope = up_call(
        place, joined, context, bias_out, gain_one, shift_one, bias_up, mid
    )
    cot = cotangent.reshape(docs * rows, width)
    layer_out, resid_two, sums_two, gw_down = down_call(
        down_place, scaled_one, active, cot, gain_one, shift_one, bias_down, gain_two, shift_two, down
    )
    resid_one, grad_ctx, sums_one, sums_up, gw_mid = ffn_back(
        place, down_place, resid_two, slope, scaled_one, inverse_one, context, gain_one, shift_one, mid, down
    )
    grad_proj, sums_proj, gw_qkv = attn_back(place, seg_count, joined, proj, grad_ctx)
    grad_text = text_grad(place, slot_ids, resid_one, [grad_proj], qkv)

    if staged:
        g_down = jnp.concatenate(join_cores(core, scatter(gw_down)), axis=0)
        low, high = join_cores(core, scatter(gw_mid))
        n = width // 2
        g_out = jnp.concatenate([low[:, :n], high[:, :n]], axis=1)
        g_up = jnp.concatenate([low[:, n:], high[:, n:]], axis=1)
        ends = join_cores(core, scatter(gw_qkv))
        g_qkv = jnp.concatenate(
            [
                ends[p % 2][:, p // 2 * 384 + t * 128 : p // 2 * 384 + t * 128 + 128]
                for t in range(3)
                for p in range(2 * GROUPS)
            ],
            axis=1,
        )
    else:
        spread = lambda g: lax.psum(
            lax.psum_scatter(g[0].astype(F32), "shard", scatter_dimension=0, tiled=True), "rep"
        )
        g_down, g_mid, g_qkv = spread(gw_down), spread(gw_mid), from_pairs(spread(gw_qkv))
        g_out, g_up = g_mid[:, :width], g_mid[:, width:]
    sums_two, sums_one, sums_up = lax.psum((sums_two, sums_one, sums_up), AXES)
    sums_proj = from_pairs(lax.psum(sums_proj, AXES).reshape(1, 3 * width))
    mine = lambda v, n: lax.dynamic_slice_in_dim(v, shard * n, n, 0)
    part = width // chips
    g_bias = jnp.concatenate([sums_proj[0, :width], sums_proj[0, 2 * width :]])
    return (
        layer_out.reshape(docs, rows, width),
        grad_text,
        g_qkv,
        mine(g_bias, 2 * part),
        g_out,
        mine(sums_one[2], part),
        mine(sums_one[0], part),
        mine(sums_one[1], part),
        g_up,
        mine(sums_up[0], up_bias.shape[0]),
        g_down,
        mine(sums_two[2], part),
        mine(sums_two[0], part),
        mine(sums_two[1], part),
    )


def solution(mesh):
    in_specs = (
        P(("rep", "shard"), None, None),
        P(("rep", "shard"), None),
        P(("rep", "shard")),
        P("shard", None),
        P("shard"),
        P("shard", None),
        P("shard"),
        P("shard"),
        P("shard"),
        P("shard", None),
        P("shard"),
        P("shard", None),
        P("shard"),
        P("shard"),
        P("shard"),
        P(("rep", "shard"), None, None),
    )
    out_specs = (
        P(("rep", "shard"), None, None),
        P(("rep", "shard"), None, None),
        P("shard", None),
        P("shard"),
        P("shard", None),
        P("shard"),
        P("shard"),
        P("shard"),
        P("shard", None),
        P("shard"),
        P("shard", None),
        P("shard"),
        P("shard"),
        P("shard"),
    )
    return jax.shard_map(body, mesh=mesh, in_specs=in_specs, out_specs=out_specs, check_vma=False)
```

time: 1140 us -> 556 us (0.49)
  matrix products: 295 us -> 0.13 us
  waiting for transfers between devices: 491 us -> 220 us
  Pallas kernels: 0 us -> 186 us
  blocking collectives: 158 us -> 0 us
  starting transfers between devices: 0.36 us -> 67.4 us
  other arithmetic: 74.5 us -> 15.1 us
  local copies, waits for them, and re-layouts: 82.8 us -> 41.9 us
  loops' own time: 12 us -> 0 us
    reduce_scatter x4 -> x0, waiting for transfers between devices: 475 us -> none  [the longest x1 177 us: body(): lax.psum_scatter(grad_w_up, 'shard', scatter_dimension=0, tiled=True)]
    dot_general x28 -> x1, matrix products: 295 us -> 0.13 us  [body(): table = jnp.dot(back.astype(F32), notes, precision=lax.Precision.HIGHEST)]
    pallas_call x0 -> x7, Pallas kernels: none -> 186 us  [the longest x1 49.8 us: attn_back(): pl.pallas_call(partial(attn_back_kernel, docs, rows), out_shape=(jax.Shap...]
    unnamed x2 -> x0, blocking collectives: 155 us -> none
    ppermute x0 -> x51, waiting for transfers between devices: none -> 115 us  [send(): return lax.ppermute(array, AXES, perm)]
    psum x1, waiting for transfers between devices: 0.01 us -> 105 us  [body(): sums_proj = from_pairs(lax.psum(sums_proj, AXES).reshape(1, 3 * width))]
    ppermute x0 -> x51, starting transfers between devices: none -> 67.3 us  [send(): return lax.ppermute(array, AXES, perm)]
    reduce_sum x10 -> x0, other arithmetic: 39.1 us -> none  [the longest x2 21.3 us: attend(): jnp.sum(jnp.exp(scores - row_top), axis=-1, keepdims=True)]
  transfers between devices with their start and end apart: 9 -> 52, of which waited for: 4 -> 21; matrix products, arithmetic and copies ran while one was open for 33% -> 7% of each run, Pallas kernels for 0% -> 12%
where the time goes in v1:
time: 556 us; the launch traced here: 546 us
  waiting for transfers between devices  220 us (40%)
  Pallas kernels  186 us (33%)
  starting transfers between devices  67.4 us (12%)
  local copies, waits for them, and re-layouts  41.9 us (8%)
  between operations  15.3 us (3%)
  other arithmetic  15.1 us (3%)
    ppermute x51, waiting for transfers between devices, send(): return lax.ppermute(array, AXES, perm)  115 us
    psum x1, waiting for transfers between devices, body(): sums_proj = from_pairs(lax.psum(sums_proj, AXES).reshape(1, 3 * width))  105 us
    ppermute x51, starting transfers between devices, send(): return lax.ppermute(array, AXES, perm)  67.3 us
    pallas_call x1, Pallas kernels, attn_back(): pl.pallas_call(partial(attn_back_kernel, docs, rows), out_shape=(jax.Shap...  49.8 us
    pallas_call x1, Pallas kernels, ffn_back(): pl.pallas_call(partial(ffn_back_kernel, len(ups), len(downs), n_rows, n_c...  44 us
    pallas_call x1, Pallas kernels, down_call(): pl.pallas_call(partial(down_kernel, len(pieces), n_rows, n_cols), out_sha...  29.1 us
    pallas_call x1, Pallas kernels, attn_fwd(): pl.pallas_call(partial(attn_fwd_kernel, docs, rows, len(pieces)), out_sha...  28.6 us
    pallas_call x1, Pallas kernels, up_call(): pl.pallas_call(partial(up_kernel, len(pieces)), out_shape=(jax.ShapeDtype...  20.1 us
  transfers between devices with their start and end apart: 52, of which 21 were waited for; matrix products, arithmetic and copies ran while one was open for 7% of the time, Pallas kernels for 12%

profile of v1, /device:TPU:0, one launch (start us, length us, event | category | flops | bytes accessed | tf_op | source)
XLA Modules:
  0.0 546.3 jit_solution(14607038687979750810)
XLA Ops:
  7.3 5.5 %concatenate.48 = bf16[576]{0:T(1024)(128)(2,1)S(1)} concatenate(bf16[96]{0:T(256)(128)(2,1)} %param.20, bf16[48]{0:T(256)(128)(2,1)} %param.22, bf16[48]{0:T(256)(128)(2,1)} %param.23, bf16[48]{0:T(256)(128)(2,1)} %param.24, bf16[192]{0:T(256)(128)(2,1)} %param.26, bf16[48]{0:T(256)(128)(2,1)} %param.28, bf16[48]{0:T(256)(128)(2,1)} %param.29, bf16[48]{0:T(256)(128)(2,1)} %param.30), dimensions={0} | concatenate | bytes 2304 | tf_op jit(solution)/shard_map/concatenate | solution.py:737
  37.9 11.1 %collective-permute-done.3.refs_5_ = bf16[4,48,1280]{2,1,0:T(8,128)(2,1)} collective-permute-done((bf16[4,48,1280]{2,1,0:T(8,128)(2,1)S(1)}, bf16[4,48,1280]{2,1,0:T(8,128)(2,1)}, u32[]{:S(2)}, u32[]{:S(2)}) %collective-permute-start.3) | collective-permute-done | bytes 491552 | tf_op jit(solution)/shard_map/ppermute | solution.py:649
  53.1 9.2 %collective-permute-start.10 = (bf16[1,48,1920]{2,1,0:T(8,128)(2,1)S(1)}, bf16[1,48,1920]{2,1,0:T(8,128)(2,1)S(1)}, u32[]{:S(2)}, u32[]{:S(2)}) collective-permute-start(bf16[1,48,1920]{2,1,0:T(8,128)(2,1)S(1)} %maximum_bitcast_fusion), channel_id=1, source_target_pairs={{0,4},{1,5},{2,6},{3,7},{4,0},{5,1},{6,2},{7,3},{8,12},{9,13},{10,... | collective-permute-start | bytes 552968 | tf_op jit(solution)/shard_map/ppermute | solution.py:649
  78.7 6.3 %collective-permute-done.23.refs_10_.refs_18_ = bf16[4,96,768]{2,1,0:T(8,128)(2,1)S(1)} collective-permute-done((bf16[4,96,768]{2,1,0:T(8,128)(2,1)S(1)}, bf16[4,96,768]{2,1,0:T(8,128)(2,1)S(1)}, u32[]{:S(2)}, u32[]{:S(2)}) %collective-permute-start.23) | collective-permute-done | bytes 589856 | tf_op jit(solution)/shard_map/ppermute | solution.py:649
  85.0 4.5 collective-permute-done.24.refs_11_.refs_19_
  89.5 11.3 %collective-permute-done.13.refs_8_.refs_10_ = bf16[4,48,1920]{2,1,0:T(8,128)(2,1)S(1)} collective-permute-done((bf16[4,48,1920]{2,1,0:T(8,128)(2,1)S(1)}, bf16[4,48,1920]{2,1,0:T(8,128)(2,1)S(1)}, u32[]{:S(2)}, u32[]{:S(2)}) %collective-permute-start.13) | collective-permute-done | bytes 737312 | tf_op jit(solution)/shard_map/ppermute | solution.py:649
  103.6 7.2 %collective-permute-done.25.refs_12_.refs_20_ = bf16[4,96,768]{2,1,0:T(8,128)(2,1)} collective-permute-done((bf16[4,96,768]{2,1,0:T(8,128)(2,1)S(1)}, bf16[4,96,768]{2,1,0:T(8,128)(2,1)}, u32[]{:S(2)}, u32[]{:S(2)}) %collective-permute-start.25) | collective-permute-done | bytes 589856 | tf_op jit(solution)/shard_map/ppermute | solution.py:649
  111.3 7.4 %collective-permute-done.15.refs_10_.refs_12_ = bf16[4,48,1920]{2,1,0:T(8,128)(2,1)} collective-permute-done((bf16[4,48,1920]{2,1,0:T(8,128)(2,1)S(1)}, bf16[4,48,1920]{2,1,0:T(8,128)(2,1)}, u32[]{:S(2)}, u32[]{:S(2)}) %collective-permute-start.15) | collective-permute-done | bytes 737312 | tf_op jit(solution)/shard_map/ppermute | solution.py:649
  126.4 28.6 %attn_fwd.1 = (bf16[3,1280,768]{2,1,0:T(8,128)(2,1)}, bf16[1280,768]{1,0:T(8,128)(2,1)}) custom-call(s32[2,32]{1,0:T(2,128)} %pad_add_fusion.refs_0_, s32[2]{0:T(128)} %refs_1_.3, bf16[1280,768]{1,0:T(8,128)(2,1)} %pool.1.refs_2_.refs_1_, f32[1,2304]{1,0:T(1,128)} %copy-done.15, bf16[4,48,1280]{2,1,0:T(8,128)(2,1)} %copy-done.4, ...), custom_call_target="tpu_custom_call" | custom-call | tf_op jit(solution)/shard_map/attn_fwd/pallas_call | solution.py:217
  155.0 20.1 %up.1 = (f32[1280,768]{1,0:T(8,128)}, f32[1280,1]{1,0:T(8,128)}, bf16[1280,3072]{1,0:T(8,128)(2,1)}, f32[1280,3072]{1,0:T(8,128)}) custom-call(s32[2,32]{1,0:T(2,128)} %pad_add_fusion.refs_0_, bf16[1280,768]{1,0:T(8,128)(2,1)} %pool.1.refs_2_.refs_1_, bf16[1280,768]{1,0:T(8,128)(2,1)} %get-tuple-element.32.refs_2_.refs_6_, f32[1,768]{1,0:T(1,128)} %reshape.292.refs_3_, ...), custom_call_target="tpu_custom_call" | custom-call | tf_op jit(solution)/shard_map/up/pallas_call | solution.py:266
  175.2 29.1 %down.1 = (bf16[1280,768]{1,0:T(8,128)(2,1)}, f32[1280,768]{1,0:T(8,128)}, f32[8,768]{1,0:T(8,128)}, bf16[32,96,768]{2,1,0:T(8,128)(2,1)}) custom-call(s32[2,32]{1,0:T(2,128)} %stack.4.refs_0_.refs_1_, f32[1280,768]{1,0:T(8,128)} %get-tuple-element.33.refs_1_.refs_4_, bf16[1280,3072]{1,0:T(8,128)(2,1)} %get-tuple-element.34.refs_2_, ...), custom_call_target="tpu_custom_call" | custom-call | tf_op jit(solution)/shard_map/down/pallas_call | solution.py:344
  204.3 44.0 %ffn_back.1 = (f32[1280,768]{1,0:T(8,128)}, bf16[1280,768]{1,0:T(8,128)(2,1)}, f32[8,768]{1,0:T(8,128)}, f32[1,3072]{1,0:T(1,128)}, bf16[32,48,1920]{2,1,0:T(8,128)(2,1)}) custom-call(s32[2,32]{1,0:T(2,128)} %pad_add_fusion.refs_0_, s32[2,32]{1,0:T(2,128)} %stack.4.refs_0_.refs_1_, f32[1280,768]{1,0:T(8,128)} %get-tuple-element.36.refs_2_, ...), custom_call_target="tpu_custom_call" | custom-call | tf_op jit(solution)/shard_map/ffn_back/pallas_call | solution.py:448
  248.3 49.8 %attn_back.1 = (bf16[3,1280,768]{2,1,0:T(8,128)(2,1)}, f32[3,1,768]{2,1,0:T(1,128)}, bf16[32,48,1152]{2,1,0:T(8,128)(2,1)}) custom-call(s32[2,32]{1,0:T(2,128)} %pad_add_fusion.refs_0_, s32[2]{0:T(128)} %refs_1_.3, bf16[1280,768]{1,0:T(8,128)(2,1)} %pool.1.refs_2_.refs_1_, bf16[3,1280,768]{2,1,0:T(8,128)(2,1)} %get-tuple-element.40.refs_3_, ...), custom_call_target="tpu_custom_call" | custom-call | tf_op jit(solution)/shard_map/attn_back/pallas_call | solution.py:554
  304.7 3.6 slice.435
  308.3 12.0 %text_grad.1 = f32[2,512,768]{2,1,0:T(8,128)} custom-call(s32[2,32]{1,0:T(2,128)} %pad_add_fusion.refs_0_, s32[2,1,512]{2,1,0:T(1,128)} %reshape.288.ids_ref.refs_1_, f32[1280,768]{1,0:T(8,128)} %get-tuple-element.39.refs_2_, bf16[3,1280,768]{2,1,0:T(8,128)(2,1)} %get-tuple-element.42.refs_3_, bf16[4,48,1280]{2,1,0:T(8,128)(2,1)} %copy-done.4, ...), custom_call_target="tpu_custom_call" | custom-call | tf_op jit(solution)/shard_map/text_grad/pallas_call | solution.py:608
  320.3 105.1 %all-reduce.6.cloned.1.call-done = (f32[1,2304]{1,0:T(1,128)}, f32[8,768]{1,0:T(8,128)}, f32[1,3072]{1,0:T(1,128)}, f32[8,768]{1,0:T(8,128)}) async-done(((f32[1,2304]{1,0:T(1,128)}, f32[8,768]{1,0:T(8,128)}, f32[1,3072]{1,0:T(1,128)}, f32[8,768]{1,0:T(8,128)}), (f32[1,2304]{1,0:T(1,128)}, f32[8,768]{1,0:T(8,128)}, f32[1,3072]{1,0:T(1,128)}, f32[8,768]{1,0:T(8,128)})) %all-reduce.6.cloned.1.call-update) | async-done | bytes 70672 | tf_op jit(solution)/shard_map/psum | solution.py:807
  437.2 8.1 %collective-permute-done.31 = bf16[8,48,1152]{2,1,0:T(8,128)(2,1)} collective-permute-done((bf16[8,48,1152]{2,1,0:T(8,128)(2,1)}, bf16[8,48,1152]{2,1,0:T(8,128)(2,1)}, u32[]{:S(2)}, u32[]{:S(2)}) %collective-permute-start.31) | collective-permute-done | bytes 884768 | tf_op jit(solution)/shard_map/ppermute | solution.py:649
  451.4 3.8 collective-permute-done.32
  455.3 4.5 collective-permute-start.33
  472.3 10.4 %collective-permute-done.45 = bf16[8,96,768]{2,1,0:T(8,128)(2,1)S(1)} collective-permute-done((bf16[8,96,768]{2,1,0:T(8,128)(2,1)S(1)}, bf16[8,96,768]{2,1,0:T(8,128)(2,1)S(1)}, u32[]{:S(2)}, u32[]{:S(2)}) %collective-permute-start.45) | collective-permute-done | bytes 1179680 | tf_op jit(solution)/shard_map/ppermute | solution.py:649
  484.6 21.6 %collective-permute-done.38 = bf16[8,48,1920]{2,1,0:T(8,128)(2,1)S(1)} collective-permute-done((bf16[8,48,1920]{2,1,0:T(8,128)(2,1)S(1)}, bf16[8,48,1920]{2,1,0:T(8,128)(2,1)S(1)}, u32[]{:S(2)}, u32[]{:S(2)}) %collective-permute-start.38) | collective-permute-done | bytes 1474592 | tf_op jit(solution)/shard_map/ppermute | solution.py:649
  508.3 4.1 collective-permute-start.47
  518.3 5.1 collective-permute-start.40
  527.9 7.5 %collective-permute-done.41 = bf16[48,1920]{1,0:T(8,128)(2,1)S(1)} collective-permute-done((bf16[48,1920]{1,0:T(8,128)(2,1)S(1)}, bf16[48,1920]{1,0:T(8,128)(2,1)S(1)}, u32[]{:S(2)}, u32[]{:S(2)}) %collective-permute-start.41) | collective-permute-done | bytes 184352 | tf_op jit(solution)/shard_map/ppermute | solution.py:649
  (253 shorter events, 111.3 us)
Async XLA Ops:
  7.2 418.1 %all-reduce.6.cloned.1.call-start = ((), (), s32[]{:S(2)}) async-start(), calls=%async_computation | async-start | bytes 141312 | tf_op jit(solution)/shard_map/psum | solution.py:807
  24.9 28.2 %collective-permute-start.20 = (bf16[1,96,768]{2,1,0:T(8,128)(2,1)S(1)}, bf16[1,96,768]{2,1,0:T(8,128)(2,1)S(1)}, u32[]{:S(2)}, u32[]{:S(2)}) collective-permute-start(bf16[1,96,768]{2,1,0:T(8,128)(2,1)S(1)} %dynamic-slice_bitcast_fusion), channel_id=1, source_target_pairs={{0,4},{1,5},{2,6},{3,7},{4,0},{5,1},{6,2},{7,3},{8,12},{9,13},{10,... | collective-permute-start | bytes 442376 | tf_op jit(solution)/shard_map/ppermute | solution.py:649
  25.9 36.4 %collective-permute-start.21 = (bf16[1,96,768]{2,1,0:T(8,128)(2,1)S(1)}, bf16[1,96,768]{2,1,0:T(8,128)(2,1)S(1)}, u32[]{:S(2)}, u32[]{:S(2)}) collective-permute-start(bf16[1,96,768]{2,1,0:T(8,128)(2,1)S(1)} %dynamic-slice_bitcast_fusion), channel_id=1, source_target_pairs={{0,8},{1,9},{2,10},{3,11},{4,12},{5,13},{6,14},{7,15},{8,0},{9,1},... | collective-permute-start | bytes 442376 | tf_op jit(solution)/shard_map/ppermute | solution.py:649
  30.3 33.9 %collective-permute-start.22 = (bf16[1,96,768]{2,1,0:T(8,128)(2,1)S(1)}, bf16[1,96,768]{2,1,0:T(8,128)(2,1)S(1)}, u32[]{:S(2)}, u32[]{:S(2)}) collective-permute-start(bf16[1,96,768]{2,1,0:T(8,128)(2,1)S(1)} %dynamic-slice_bitcast_fusion), channel_id=1, source_target_pairs={{0,12},{1,13},{2,14},{3,15},{4,8},{5,9},{6,10},{7,11},{8,4},{9,5},... | collective-permute-start | bytes 442376 | tf_op jit(solution)/shard_map/ppermute | solution.py:649
  36.4 38.1 %collective-permute-start.4 = (bf16[4,48,1280]{2,1,0:T(8,128)(2,1)S(1)}, bf16[4,48,1280]{2,1,0:T(8,128)(2,1)S(1)}, u32[]{:S(2)}, u32[]{:S(2)}) collective-permute-start(bf16[4,48,1280]{2,1,0:T(8,128)(2,1)S(1)} %pad_maximum_fusion.4.refs_4_), channel_id=1, source_target_pairs={{0,2},{1,3},{2,0},{3,1},{4,6},{5,7},{6,4},{7,5},{8,10},{9,11},{10,... | collective-permute-start | bytes 1474568 | tf_op jit(solution)/shard_map/ppermute | solution.py:649
  49.1 26.9 %collective-permute-start.5 = (bf16[4,48,1280]{2,1,0:T(8,128)(2,1)}, bf16[4,48,1280]{2,1,0:T(8,128)(2,1)}, u32[]{:S(2)}, u32[]{:S(2)}) collective-permute-start(bf16[4,48,1280]{2,1,0:T(8,128)(2,1)} %collective-permute-done.3.refs_5_), channel_id=1, source_target_pairs={{0,2},{1,3},{2,0},{3,1},{4,6},{5,7},{6,4},{7,5},{8,10},{9,11},{10,... | collective-permute-start | bytes 1474568 | tf_op jit(solution)/shard_map/ppermute | solution.py:649
  73.1 16.4 %collective-permute-start.24 = (bf16[4,96,768]{2,1,0:T(8,128)(2,1)S(1)}, bf16[4,96,768]{2,1,0:T(8,128)(2,1)}, u32[]{:S(2)}, u32[]{:S(2)}) collective-permute-start(bf16[4,96,768]{2,1,0:T(8,128)(2,1)S(1)} %pad_maximum_fusion.1.refs_9_.refs_17_), channel_id=1, source_target_pairs={{0,2},{1,3},{2,0},{3,1},{4,6},{5,7},{6,4},{7,5},{8,10},{9,11},{10,... | collective-permute-start | bytes 1769480 | tf_op jit(solution)/shard_map/ppermute | solution.py:649
  74.5 26.3 %collective-permute-start.13 = (bf16[4,48,1920]{2,1,0:T(8,128)(2,1)S(1)}, bf16[4,48,1920]{2,1,0:T(8,128)(2,1)S(1)}, u32[]{:S(2)}, u32[]{:S(2)}) collective-permute-start(bf16[4,48,1920]{2,1,0:T(8,128)(2,1)S(1)} %pad_maximum_fusion.refs_7_.refs_9_), channel_id=1, source_target_pairs={{0,1},{1,0},{2,3},{3,2},{4,5},{5,4},{6,7},{7,6},{8,9},{9,8},{10,11... | collective-permute-start | bytes 2211848 | tf_op jit(solution)/shard_map/ppermute | solution.py:649
  76.0 25.3 %collective-permute-start.14 = (bf16[4,48,1920]{2,1,0:T(8,128)(2,1)S(1)}, bf16[4,48,1920]{2,1,0:T(8,128)(2,1)}, u32[]{:S(2)}, u32[]{:S(2)}) collective-permute-start(bf16[4,48,1920]{2,1,0:T(8,128)(2,1)S(1)} %pad_maximum_fusion.refs_7_.refs_9_), channel_id=1, source_target_pairs={{0,2},{1,3},{2,0},{3,1},{4,6},{5,7},{6,4},{7,5},{8,10},{9,11},{10,... | collective-permute-start | bytes 2211848 | tf_op jit(solution)/shard_map/ppermute | solution.py:649
  78.6 24.3 %collective-permute-start.16 = (bf16[4,48,1920]{2,1,0:T(8,128)(2,1)S(1)}, bf16[4,48,1920]{2,1,0:T(8,128)(2,1)S(1)}, u32[]{:S(2)}, u32[]{:S(2)}) collective-permute-start(bf16[4,48,1920]{2,1,0:T(8,128)(2,1)S(1)} %pad_maximum_fusion.refs_7_.refs_9_), channel_id=1, source_target_pairs={{0,16},{1,17},{2,18},{3,19},{4,20},{5,21},{6,22},{7,23},{8,24},{9,... | collective-permute-start | bytes 2211848 | tf_op jit(solution)/shard_map/ppermute | solution.py:649
  85.0 17.8 %collective-permute-start.7 = (bf16[4,48,1280]{2,1,0:T(8,128)(2,1)}, bf16[4,48,1280]{2,1,0:T(8,128)(2,1)S(1)}, u32[]{:S(2)}, u32[]{:S(2)}) collective-permute-start(bf16[4,48,1280]{2,1,0:T(8,128)(2,1)} %collective-permute-done.3.refs_5_), channel_id=1, source_target_pairs={{0,16},{1,17},{2,18},{3,19},{4,20},{5,21},{6,22},{7,23},{8,24},{9,... | collective-permute-start | bytes 1474568 | tf_op jit(solution)/shard_map/ppermute | solution.py:649
  101.3 17.4 %collective-permute-start.15 = (bf16[4,48,1920]{2,1,0:T(8,128)(2,1)S(1)}, bf16[4,48,1920]{2,1,0:T(8,128)(2,1)}, u32[]{:S(2)}, u32[]{:S(2)}) collective-permute-start(bf16[4,48,1920]{2,1,0:T(8,128)(2,1)S(1)} %collective-permute-done.13.refs_8_.refs_10_), channel_id=1, source_target_pairs={{0,2},{1,3},{2,0},{3,1},{4,6},{5,7},{6,4},{7,5},{8,10},{9,11},{10,... | collective-permute-start | bytes 2211848 | tf_op jit(solution)/shard_map/ppermute | solution.py:649
  102.9 16.7 %collective-permute-start.18 = (bf16[4,48,1920]{2,1,0:T(8,128)(2,1)}, bf16[4,48,1920]{2,1,0:T(8,128)(2,1)S(1)}, u32[]{:S(2)}, u32[]{:S(2)}) collective-permute-start(bf16[4,48,1920]{2,1,0:T(8,128)(2,1)} %collective-permute-done.14.refs_9_.refs_11_), channel_id=1, source_target_pairs={{0,16},{1,17},{2,18},{3,19},{4,20},{5,21},{6,22},{7,23},{8,24},{9,... | collective-permute-start | bytes 2211848 | tf_op jit(solution)/shard_map/ppermute | solution.py:649
  110.8 64.3 %collective-permute-start.26 = (bf16[4,96,768]{2,1,0:T(8,128)(2,1)S(1)}, bf16[4,96,768]{2,1,0:T(8,128)(2,1)}, u32[]{:S(2)}, u32[]{:S(2)}) collective-permute-start(bf16[4,96,768]{2,1,0:T(8,128)(2,1)S(1)} %pad_maximum_fusion.1.refs_9_.refs_17_), channel_id=1, source_target_pairs={{0,16},{1,17},{2,18},{3,19},{4,20},{5,21},{6,22},{7,23},{8,24},{9,... | collective-permute-start | bytes 1769480 | tf_op jit(solution)/shard_map/ppermute | solution.py:649
  110.8 64.3 %collective-permute-start.27 = (bf16[4,96,768]{2,1,0:T(8,128)(2,1)S(1)}, bf16[4,96,768]{2,1,0:T(8,128)(2,1)}, u32[]{:S(2)}, u32[]{:S(2)}) collective-permute-start(bf16[4,96,768]{2,1,0:T(8,128)(2,1)S(1)} %collective-permute-done.23.refs_10_.refs_18_), channel_id=1, source_target_pairs={{0,16},{1,17},{2,18},{3,19},{4,20},{5,21},{6,22},{7,23},{8,24},{9,... | collective-permute-start | bytes 1769480 | tf_op jit(solution)/shard_map/ppermute | solution.py:649
  118.7 56.5 %collective-permute-start.28 = (bf16[4,96,768]{2,1,0:T(8,128)(2,1)}, bf16[4,96,768]{2,1,0:T(8,128)(2,1)}, u32[]{:S(2)}, u32[]{:S(2)}) collective-permute-start(bf16[4,96,768]{2,1,0:T(8,128)(2,1)} %collective-permute-done.24.refs_11_.refs_19_), channel_id=1, source_target_pairs={{0,16},{1,17},{2,18},{3,19},{4,20},{5,21},{6,22},{7,23},{8,24},{9,... | collective-permute-start | bytes 1769480 | tf_op jit(solution)/shard_map/ppermute | solution.py:649
  118.7 56.4 %collective-permute-start.29 = (bf16[4,96,768]{2,1,0:T(8,128)(2,1)}, bf16[4,96,768]{2,1,0:T(8,128)(2,1)}, u32[]{:S(2)}, u32[]{:S(2)}) collective-permute-start(bf16[4,96,768]{2,1,0:T(8,128)(2,1)} %collective-permute-done.25.refs_12_.refs_20_), channel_id=1, source_target_pairs={{0,16},{1,17},{2,18},{3,19},{4,20},{5,21},{6,22},{7,23},{8,24},{9,... | collective-permute-start | bytes 1769480 | tf_op jit(solution)/shard_map/ppermute | solution.py:649
  120.5 34.5 %collective-permute-start.19 = (bf16[4,48,1920]{2,1,0:T(8,128)(2,1)}, bf16[4,48,1920]{2,1,0:T(8,128)(2,1)}, u32[]{:S(2)}, u32[]{:S(2)}) collective-permute-start(bf16[4,48,1920]{2,1,0:T(8,128)(2,1)} %collective-permute-done.15.refs_10_.refs_12_), channel_id=1, source_target_pairs={{0,16},{1,17},{2,18},{3,19},{4,20},{5,21},{6,22},{7,23},{8,24},{9,... | collective-permute-start | bytes 2211848 | tf_op jit(solution)/shard_map/ppermute | solution.py:649
  300.8 127.8 %collective-permute-start.30 = (bf16[16,48,1152]{2,1,0:T(8,128)(2,1)}, bf16[16,48,1152]{2,1,0:T(8,128)(2,1)}, u32[]{:S(2)}, u32[]{:S(2)}) collective-permute-start(bf16[16,48,1152]{2,1,0:T(8,128)(2,1)} %slice.389), channel_id=1, source_target_pairs={{0,16},{1,17},{2,18},{3,19},{4,20},{5,21},{6,22},{7,23},{8,24},{9,... | collective-permute-start | bytes 5308424 | tf_op jit(solution)/shard_map/ppermute | solution.py:649
  304.2 158.1 %collective-permute-start.44 = (bf16[16,96,768]{2,1,0:T(8,128)(2,1)}, bf16[16,96,768]{2,1,0:T(8,128)(2,1)S(1)}, u32[]{:S(2)}, u32[]{:S(2)}) collective-permute-start(bf16[16,96,768]{2,1,0:T(8,128)(2,1)} %slice.458), channel_id=1, source_target_pairs={{0,16},{1,17},{2,18},{3,19},{4,20},{5,21},{6,22},{7,23},{8,24},{9,... | collective-permute-start | bytes 7077896 | tf_op jit(solution)/shard_map/ppermute | solution.py:649
  308.3 159.6 %collective-permute-start.37 = (bf16[16,48,1920]{2,1,0:T(8,128)(2,1)}, bf16[16,48,1920]{2,1,0:T(8,128)(2,1)}, u32[]{:S(2)}, u32[]{:S(2)}) collective-permute-start(bf16[16,48,1920]{2,1,0:T(8,128)(2,1)} %slice.435), channel_id=1, source_target_pairs={{0,16},{1,17},{2,18},{3,19},{4,20},{5,21},{6,22},{7,23},{8,24},{9,... | collective-permute-start | bytes 8847368 | tf_op jit(solution)/shard_map/ppermute | solution.py:649
  464.6 18.1 %collective-permute-start.45 = (bf16[8,96,768]{2,1,0:T(8,128)(2,1)S(1)}, bf16[8,96,768]{2,1,0:T(8,128)(2,1)S(1)}, u32[]{:S(2)}, u32[]{:S(2)}) collective-permute-start(bf16[8,96,768]{2,1,0:T(8,128)(2,1)S(1)} %get-tuple-element.57), channel_id=1, source_target_pairs={{0,2},{1,3},{2,0},{3,1},{4,6},{5,7},{6,4},{7,5},{8,10},{9,11},{10,... | collective-permute-start | bytes 3538952 | tf_op jit(solution)/shard_map/ppermute | solution.py:649
  470.5 35.7 %collective-permute-start.38 = (bf16[8,48,1920]{2,1,0:T(8,128)(2,1)S(1)}, bf16[8,48,1920]{2,1,0:T(8,128)(2,1)S(1)}, u32[]{:S(2)}, u32[]{:S(2)}) collective-permute-start(bf16[8,48,1920]{2,1,0:T(8,128)(2,1)S(1)} %get-tuple-element.55), channel_id=1, source_target_pairs={{0,2},{1,3},{2,0},{3,1},{4,6},{5,7},{6,4},{7,5},{8,10},{9,11},{10,... | collective-permute-start | bytes 4423688 | tf_op jit(solution)/shard_map/ppermute | solution.py:649
  483.0 25.1 %collective-permute-start.46 = (bf16[4,96,768]{2,1,0:T(8,128)(2,1)S(1)}, bf16[4,96,768]{2,1,0:T(8,128)(2,1)S(1)}, u32[]{:S(2)}, u32[]{:S(2)}) collective-permute-start(bf16[4,96,768]{2,1,0:T(8,128)(2,1)S(1)} %get-tuple-element.63), channel_id=1, source_target_pairs={{0,1},{1,0},{2,3},{3,2},{4,5},{5,4},{6,7},{7,6},{8,9},{9,8},{10,11... | collective-permute-start | bytes 1769480 | tf_op jit(solution)/shard_map/ppermute | solution.py:649
  (48 other events, 848.2 us)
Sparse Core Ops, SparseCore 0:
  301.0 124.3 all-reduce.5
